TPU v7x, 32 devices: a whole 2x2x4 slice. The times are simulated.
32 devices in a mesh: dp: 16 (over z, x, core), seq: 2 (over y).
Axes of the slice: x: 2, y: 2, z: 4, core: 2. Of those that a mesh axis runs over, the one named last changes fastest.
Arguments:
- captions: bfloat16 [16, 1024, 768], P('dp', 'seq'), may hold values from -6 to 6
- patches: bfloat16 [16, 196, 768], P('dp', 'seq'), may hold values from -32 to 32, as said below
- prefix: bfloat16 [16, 32, 768], P('dp', 'seq'), may hold values from -6 to 6
- prefix_count: int32 [16], P('dp'), may hold values from 0 to 32, as said below
- caption_len: int32 [16], P('dp'), may hold values from 513 to 1024, as said below
- cotangent: bfloat16 [16, 1024, 768], P('dp', 'seq'), may hold values from -6 to 6
- w_patch: bfloat16 [768, 768], P('dp'), may hold values from -0.21875 to 0.21875
- w_conv: bfloat16 [2, 6912, 768], P(None, 'dp'), may hold values from -0.078125 to 0.078125
- w_self_qkv: bfloat16 [768, 2304], P('dp'), may hold values from -0.21875 to 0.21875
- w_self_out: bfloat16 [768, 768], P('dp'), may hold values from -3.5 to 3.5
- w_cross_q: bfloat16 [768, 768], P('dp'), may hold values from -0.21875 to 0.21875
- w_cross_kv: bfloat16 [768, 1536], P('dp'), may hold values from -0.21875 to 0.21875
- w_cross_out: bfloat16 [768, 768], P('dp'), may hold values from -1.75 to 1.75
- w_up: bfloat16 [768, 3072], P('dp'), may hold values from -0.21875 to 0.21875
- w_down: bfloat16 [3072, 768], P('dp'), may hold values from -0.109375 to 0.109375
- norm_params: bfloat16 [12, 768], P(None, 'dp'), may hold values from 0.25 to 1.75
Outputs:
- block_output: bfloat16 [16, 1024, 768], P('dp', 'seq')
- caption_grad: bfloat16 [16, 1024, 768], P('dp', 'seq')
- prefix_grad: bfloat16 [16, 32, 768], P('dp', 'seq')
- grad_w_patch: float32 [768, 768], P('dp')
- grad_w_conv: float32 [2, 6912, 768], P(None, 'dp')
- grad_w_self_qkv: float32 [768, 2304], P('dp')
- grad_w_self_out: float32 [768, 768], P('dp')
- grad_w_cross_q: float32 [768, 768], P('dp')
- grad_w_cross_kv: float32 [768, 1536], P('dp')
- grad_w_cross_out: float32 [768, 768], P('dp')
- grad_w_up: float32 [768, 3072], P('dp')
- grad_w_down: float32 [3072, 768], P('dp')
- grad_norm_params: float32 [12, 768], P(None, 'dp')
Inputs may be any that keep to these rules, and one draw needn't show every extreme that they name: `prefix_count`: each example has between 0 and 32 live prefix slots; some example has all 32 and some none. `caption_len`: every caption reaches past the first 512 slots; some caption fills all 1024 slots. `patches`: pixel values; each example has its own overall scale.
All inputs are finite; a program needn't handle non-finite values.
Results may differ from a plain program's by a relative error of at most 0.035.
Values may be sent and summed in bfloat16 or wider, within the bound.
A program may use at most 384 MiB of HBM per device.

v0:
```python
import jax
import jax.numpy as jnp
from jax import lax
from jax.sharding import PartitionSpec as P

HEADS = 12
SIDE = 14


def padded_2(cells, sides, width):
    for axis, dim in sides:
        count = lax.axis_size(axis)
        ends = count - 1
        head = lax.slice_in_dim(cells, 0, width, axis=dim)
        tail = lax.slice_in_dim(cells, cells.shape[dim] - width, cells.shape[dim], axis=dim)
        cells = jnp.concatenate(
            [
                lax.ppermute(tail, axis, [(i, (i + 1) % count) for i in range(ends)]),
                cells,
                lax.ppermute(head, axis, [((i + 1) % count, i) for i in range(ends)]),
            ],
            axis=dim,
        )
    return cells


def passed_along(array, axis, by):
    length = lax.axis_size(axis)
    pairs = [(i, i + by) for i in range(length) if 0 <= i + by < length]
    return lax.ppermute(array, axis, pairs)


def layer_norm(activ, gain_vec, bias_vec):
    row_mean = jnp.mean(activ, -1, keepdims=True)
    centred = activ - row_mean
    spread = jnp.mean(centred * centred, -1, keepdims=True)
    return centred * lax.rsqrt(spread + 1e-06) * gain_vec + bias_vec


def heads_of(matrix):
    return matrix.reshape(matrix.shape[0], HEADS, -1)


def dot_float(left, right):
    return jnp.dot(left, right, preferred_element_type=jnp.float32)


def norm_batch(values, gain_vec, bias_vec, number):
    sums = lax.psum((jnp.sum(values, 0), jnp.sum(values * values, 0)), ("dp", "seq"))
    col_mean = sums[0] / number
    col_var = sums[1] / number - col_mean * col_mean
    inv_std = lax.rsqrt(col_var + 1e-05)
    normed = (values - col_mean) * inv_std
    return (normed, inv_std, normed * gain_vec + bias_vec)


def batch_back(d_pre, normed, inv_std, gain_vec, number):
    grad_gain = jnp.sum(d_pre * normed, 0)
    grad_bias = jnp.sum(d_pre, 0)
    d_normed = d_pre * gain_vec
    sums = lax.psum((jnp.sum(d_normed, 0), jnp.sum(d_normed * normed, 0)), ("dp", "seq"))
    d_values = inv_std * (d_normed - sums[0] / number - normed * (sums[1] / number))
    return (d_values, grad_gain, grad_bias)


def conv_fwd(flat_low, weight):
    features = flat_low.shape[1]
    grid_rows = flat_low.shape[0] // SIDE
    grid = flat_low.reshape(grid_rows, SIDE, features)
    padded = padded_2(grid, (("seq", 0),), 1)
    padded = jnp.pad(padded, ((0, 0), (1, 1), (0, 0)))
    total = jnp.zeros((grid_rows * SIDE, features), jnp.float32)
    for row_tap in range(3):
        for col_tap in range(3):
            tap = 3 * row_tap + col_tap
            window = padded[row_tap : row_tap + grid_rows, col_tap : col_tap + SIDE].reshape(
                -1, features
            )
            total = total + dot_float(window, weight[tap * features : (tap + 1) * features])
    return (total, padded)


def send_rim(rim_rows, offset):
    return passed_along(rim_rows.astype(jnp.bfloat16), "seq", offset).astype(rim_rows.dtype)


def conv_back(padded, d_out_low, weight):
    features = d_out_low.shape[1]
    grid_rows = padded.shape[0] - 2
    d_padded = jnp.zeros((grid_rows + 2, SIDE + 2, features), jnp.float32)
    tap_grads = []
    for row_tap in range(3):
        for col_tap in range(3):
            tap = 3 * row_tap + col_tap
            tap_weight = weight[tap * features : (tap + 1) * features]
            window = padded[row_tap : row_tap + grid_rows, col_tap : col_tap + SIDE].reshape(
                -1, features
            )
            tap_grads.append(dot_float(window.T, d_out_low))
            spread = dot_float(d_out_low, tap_weight.T).reshape(grid_rows, SIDE, features)
            d_padded = d_padded + jnp.pad(
                spread, ((row_tap, 2 - row_tap), (col_tap, 2 - col_tap), (0, 0))
            )
    inner = d_padded[1 : grid_rows + 1, 1 : SIDE + 1]
    from_below = send_rim(d_padded[0, 1 : SIDE + 1], -1)
    from_above = send_rim(d_padded[grid_rows + 1, 1 : SIDE + 1], 1)
    inner = inner.at[grid_rows - 1].add(from_below).at[0].add(from_above)
    return (jnp.concatenate(tap_grads, 0), inner.reshape(-1, features))


def attend_block(queries, key_rows, value_rows, allowed, score_scale):
    scores = (
        jnp.einsum("qhd,khd->hqk", queries, key_rows, preferred_element_type=jnp.float32)
        * score_scale
    )
    scores = jnp.where(allowed[None], scores, -1000000000.0)
    row_max = jnp.max(scores, -1, keepdims=True)
    exponent = jnp.exp(scores - row_max)
    row_total = jnp.sum(exponent, -1, keepdims=True)
    softmax = (exponent / row_total).astype(jnp.bfloat16)
    outputs = jnp.einsum("hqk,khd->qhd", softmax, value_rows, preferred_element_type=jnp.float32)
    return (outputs, row_max + jnp.log(row_total))


def attend_back(queries, key_rows, value_rows, allowed, score_scale, grad_out, log_total):
    scores = (
        jnp.einsum("qhd,khd->hqk", queries, key_rows, preferred_element_type=jnp.float32)
        * score_scale
    )
    scores = jnp.where(allowed[None], scores, -1000000000.0)
    softmax = jnp.exp(scores - log_total)
    d_softmax = jnp.einsum("qhd,khd->hqk", grad_out, value_rows, preferred_element_type=jnp.float32)
    row_delta = jnp.sum(softmax * d_softmax, -1, keepdims=True)
    d_scores = (softmax * (d_softmax - row_delta)).astype(jnp.bfloat16)
    d_query = (
        jnp.einsum("hqk,khd->qhd", d_scores, key_rows, preferred_element_type=jnp.float32)
        * score_scale
    )
    d_keys = (
        jnp.einsum("hqk,qhd->khd", d_scores, queries, preferred_element_type=jnp.float32)
        * score_scale
    )
    d_values = jnp.einsum(
        "hqk,qhd->khd", softmax.astype(jnp.bfloat16), grad_out, preferred_element_type=jnp.float32
    )
    return (d_query, d_keys, d_values)


def run_attention(queries, key_rows, value_rows, allow_fn, score_scale):
    row_count = queries.shape[0]
    block_rows = min(512, row_count)
    block_count = row_count // block_rows
    query_blocks = queries.reshape(block_count, block_rows, queries.shape[1], queries.shape[2])
    starts = jnp.arange(block_count, dtype=jnp.int32) * block_rows

    def one_block(block_pair):
        return attend_block(
            block_pair[0], key_rows, value_rows, allow_fn(block_pair[1], block_rows), score_scale
        )

    outputs, log_total = lax.map(one_block, (query_blocks, starts))
    return (outputs.reshape(queries.shape), log_total)


def run_back(queries, key_rows, value_rows, allow_fn, score_scale, grad_out, log_total):
    row_count = queries.shape[0]
    block_rows = min(512, row_count)
    block_count = row_count // block_rows
    query_blocks = queries.reshape(block_count, block_rows, queries.shape[1], queries.shape[2])
    grad_blocks = grad_out.reshape(query_blocks.shape)
    starts = jnp.arange(block_count, dtype=jnp.int32) * block_rows

    def one_block(running, block_items):
        query_part, grad_part, total_part, first_row = block_items
        d_query, d_keys, d_values = attend_back(
            query_part,
            key_rows,
            value_rows,
            allow_fn(first_row, block_rows),
            score_scale,
            grad_part,
            total_part,
        )
        return ((running[0] + d_keys, running[1] + d_values), d_query)

    zero_grads = jnp.zeros(key_rows.shape, jnp.float32)
    sums_kv, d_query = lax.scan(
        one_block, (zero_grads, zero_grads), (query_blocks, grad_blocks, log_total, starts)
    )
    return (d_query.reshape(queries.shape), sums_kv[0], sums_kv[1])


def on_device(
    captions,
    patches,
    prefix,
    prefix_count,
    caption_len,
    cotangent,
    w_patch,
    w_conv,
    w_self_qkv,
    w_self_out,
    w_cross_q,
    w_cross_kv,
    w_cross_out,
    w_up,
    w_down,
    norm_params,
):
    gathered = (
        lax.all_gather(w_patch, "dp", axis=0, tiled=True),
        lax.all_gather(w_conv, "dp", axis=1, tiled=True),
        lax.all_gather(w_self_qkv, "dp", axis=0, tiled=True),
        lax.all_gather(w_self_out, "dp", axis=0, tiled=True),
        lax.all_gather(w_cross_q, "dp", axis=0, tiled=True),
        lax.all_gather(w_cross_kv, "dp", axis=0, tiled=True),
        lax.all_gather(w_cross_out, "dp", axis=0, tiled=True),
        lax.all_gather(w_up, "dp", axis=0, tiled=True),
        lax.all_gather(w_down, "dp", axis=0, tiled=True),
        lax.all_gather(norm_params, "dp", axis=1, tiled=True),
    )
    (
        full_patch,
        full_conv,
        full_qkv,
        full_sout,
        full_cq,
        full_ckv,
        full_cout,
        full_up,
        full_down,
        full_norms,
    ) = gathered
    norms = full_norms.astype(jnp.float32)
    features = full_sout.shape[0]
    score_scale = (features // HEADS) ** (-0.5)
    seq_count = lax.axis_size("seq")
    seq_index = lax.axis_index("seq")
    pixels = patches[0]
    stem_out = dot_float(pixels, full_patch)
    number = stem_out.shape[0] * lax.axis_size("dp") * seq_count
    normed_one, inv_one, pre_one = norm_batch(stem_out, norms[0], norms[1], number)
    first_out = jax.nn.gelu(pre_one)
    first_low = first_out.astype(jnp.bfloat16)
    conv_two, padded_two = conv_fwd(first_low, full_conv[0])
    normed_two, inv_two, pre_two = norm_batch(conv_two, norms[2], norms[3], number)
    second_out = first_out + jax.nn.gelu(pre_two)
    second_low = second_out.astype(jnp.bfloat16)
    conv_three, padded_three = conv_fwd(second_low, full_conv[1])
    normed_three, inv_three, pre_three = norm_batch(conv_three, norms[4], norms[5], number)
    third_out = second_out + jax.nn.gelu(pre_three)
    patch_low = third_out.astype(jnp.bfloat16)
    prefix_low = prefix[0]
    kv_prefix = dot_float(prefix_low, full_ckv).astype(jnp.bfloat16)
    kv_patch = dot_float(patch_low, full_ckv).astype(jnp.bfloat16)
    all_prefix, all_patch = (
        lax.all_gather(kv_prefix, "seq", axis=0, tiled=True),
        lax.all_gather(kv_patch, "seq", axis=0, tiled=True),
    )
    memory_kv = jnp.concatenate([all_prefix, all_patch], 0)
    mem_rows = memory_kv.shape[0]
    prefix_total = all_prefix.shape[0]
    mem_keys = heads_of(memory_kv[:, :features])
    mem_values = heads_of(memory_kv[:, features:])
    slot_ids = jnp.arange(mem_rows, dtype=jnp.int32)
    mem_allowed = (slot_ids >= prefix_total) | (slot_ids < prefix_count[0])

    def cross_allow(first_row, block_rows):
        return jnp.broadcast_to(mem_allowed[None], (block_rows, mem_rows))

    inputs = captions[0].astype(jnp.float32)
    row_count = inputs.shape[0]
    low_one = layer_norm(inputs, norms[6], norms[7]).astype(jnp.bfloat16)
    qkv = dot_float(low_one, full_qkv).astype(jnp.bfloat16)
    queries = heads_of(qkv[:, :features])
    own_keys = heads_of(qkv[:, features : 2 * features])
    own_values = heads_of(qkv[:, 2 * features :])
    key_parts = [own_keys]
    value_parts = [own_values]
    position_parts = [seq_index * row_count + jnp.arange(row_count, dtype=jnp.int32)]
    offset = 1
    got_keys, got_values = passed_along((own_keys, own_values), "seq", offset)
    key_parts.insert(0, got_keys)
    value_parts.insert(0, got_values)
    position_parts.insert(
        0, (seq_index - offset) * row_count + jnp.arange(row_count, dtype=jnp.int32)
    )
    all_keys = jnp.concatenate(key_parts, 0)
    all_values = jnp.concatenate(value_parts, 0)
    key_pos = jnp.concatenate(position_parts, 0)
    length_one = caption_len[0]

    def self_allow(first_row, block_rows):
        query_pos = seq_index * row_count + first_row + jnp.arange(block_rows, dtype=jnp.int32)
        return (
            (key_pos[None] <= query_pos[:, None])
            & (key_pos[None] >= 0)
            & (key_pos[None] < length_one)
        )

    self_out, self_total = run_attention(queries, all_keys, all_values, self_allow, score_scale)
    self_low = self_out.reshape(row_count, features).astype(jnp.bfloat16)
    after_self = inputs + dot_float(self_low, full_sout)
    low_two = layer_norm(after_self, norms[8], norms[9]).astype(jnp.bfloat16)
    cross_flat = dot_float(low_two, full_cq).astype(jnp.bfloat16)
    cross_q = heads_of(cross_flat)
    cross_out, cross_total = run_attention(cross_q, mem_keys, mem_values, cross_allow, score_scale)
    cross_low = cross_out.reshape(row_count, features).astype(jnp.bfloat16)
    after_cross = after_self + dot_float(cross_low, full_cout)
    low_three = layer_norm(after_cross, norms[10], norms[11]).astype(jnp.bfloat16)
    up_proj = dot_float(low_three, full_up)
    hidden_low = jax.nn.gelu(up_proj).astype(jnp.bfloat16)
    result = after_cross + dot_float(hidden_low, full_down)
    back_weights = (
        lax.all_gather(w_patch, "dp", axis=0, tiled=True),
        lax.all_gather(w_conv, "dp", axis=1, tiled=True),
        lax.all_gather(w_self_qkv, "dp", axis=0, tiled=True),
        lax.all_gather(w_self_out, "dp", axis=0, tiled=True),
        lax.all_gather(w_cross_q, "dp", axis=0, tiled=True),
        lax.all_gather(w_cross_kv, "dp", axis=0, tiled=True),
        lax.all_gather(w_cross_out, "dp", axis=0, tiled=True),
        lax.all_gather(w_up, "dp", axis=0, tiled=True),
        lax.all_gather(w_down, "dp", axis=0, tiled=True),
        lax.all_gather(norm_params, "dp", axis=1, tiled=True),
    )
    (
        back_patch,
        back_conv,
        back_qkv,
        back_sout,
        back_cq,
        back_ckv,
        back_cout,
        back_up,
        back_down,
        back_norms,
    ) = back_weights
    bnorms = back_norms.astype(jnp.float32)
    out_grad = cotangent[0].astype(jnp.float32)
    grad_low = cotangent[0]
    grad_down = dot_float(hidden_low.T, grad_low)
    d_hidden = dot_float(grad_low, back_down.T)
    unused_gelu, gelu_back = jax.vjp(jax.nn.gelu, up_proj)
    d_upper = gelu_back(d_hidden)[0].astype(jnp.bfloat16)
    grad_up = dot_float(low_three.T, d_upper)
    unused_three, norm_back_three = jax.vjp(layer_norm, after_cross, bnorms[10], bnorms[11])
    d_three, grad_gain_three, grad_bias_three = norm_back_three(dot_float(d_upper, back_up.T))
    d_after_cross = out_grad + d_three
    cross_grad_low = d_after_cross.astype(jnp.bfloat16)
    grad_cout = dot_float(cross_low.T, cross_grad_low)
    d_cross = heads_of(dot_float(cross_grad_low, back_cout.T).astype(jnp.bfloat16))
    d_cross_q, d_mem_keys, d_mem_values = run_back(
        cross_q, mem_keys, mem_values, cross_allow, score_scale, d_cross, cross_total
    )
    d_cross_low = d_cross_q.reshape(row_count, features).astype(jnp.bfloat16)
    grad_cq = dot_float(low_two.T, d_cross_low)
    unused_two, norm_back_two = jax.vjp(layer_norm, after_self, bnorms[8], bnorms[9])
    d_two, grad_gain_two, grad_bias_two = norm_back_two(dot_float(d_cross_low, back_cq.T))
    d_after_self = d_after_cross + d_two
    d_memory = jnp.concatenate(
        [d_mem_keys.reshape(mem_rows, features), d_mem_values.reshape(mem_rows, features)], 1
    )
    mine_prefix, mine_patch = (
        lax.psum_scatter(
            d_memory[:prefix_total].astype(jnp.bfloat16), "seq", scatter_dimension=0, tiled=True
        ).astype(jnp.float32),
        lax.psum_scatter(
            d_memory[prefix_total:].astype(jnp.bfloat16), "seq", scatter_dimension=0, tiled=True
        ).astype(jnp.float32),
    )
    mine_prefix_low = mine_prefix.astype(jnp.bfloat16)
    mine_patch_low = mine_patch.astype(jnp.bfloat16)
    grad_ckv = dot_float(prefix_low.T, mine_prefix_low) + dot_float(patch_low.T, mine_patch_low)
    prefix_back = dot_float(mine_prefix_low, back_ckv.T)
    d_third = dot_float(mine_patch_low, back_ckv.T)
    unused_act_three, act_back_three = jax.vjp(jax.nn.gelu, pre_three)
    d_conv_three, grad_gain_bn3, grad_bias_bn3 = batch_back(
        act_back_three(d_third)[0], normed_three, inv_three, bnorms[4], number
    )
    grad_conv_one, d_second_in = conv_back(
        padded_three, d_conv_three.astype(jnp.bfloat16), back_conv[1]
    )
    d_second = d_third + d_second_in
    unused_act_two, act_back_two = jax.vjp(jax.nn.gelu, pre_two)
    d_conv_two, grad_gain_bn2, grad_bias_bn2 = batch_back(
        act_back_two(d_second)[0], normed_two, inv_two, bnorms[2], number
    )
    grad_conv_zero, d_first_in = conv_back(
        padded_two, d_conv_two.astype(jnp.bfloat16), back_conv[0]
    )
    d_first = d_second + d_first_in
    unused_act_one, act_back_one = jax.vjp(jax.nn.gelu, pre_one)
    d_stem, grad_gain_bn1, grad_bias_bn1 = batch_back(
        act_back_one(d_first)[0], normed_one, inv_one, bnorms[0], number
    )
    grad_patch = dot_float(pixels.T, d_stem.astype(jnp.bfloat16))
    grad_conv = jnp.stack([grad_conv_zero, grad_conv_one])
    self_grad_low = d_after_self.astype(jnp.bfloat16)
    grad_sout = dot_float(self_low.T, self_grad_low)
    d_self = heads_of(dot_float(self_grad_low, back_sout.T).astype(jnp.bfloat16))
    d_query, d_all_keys, d_all_values = run_back(
        queries, all_keys, all_values, self_allow, score_scale, d_self, self_total
    )
    own_start = (seq_count - 1) * row_count
    own_dkeys = d_all_keys[own_start:]
    own_dvalues = d_all_values[own_start:]
    offset = 1
    piece_start = (seq_count - 1 - offset) * row_count
    back_keys = passed_along(
        d_all_keys[piece_start : piece_start + row_count].astype(jnp.bfloat16), "seq", -offset
    ).astype(jnp.float32)
    back_values = passed_along(
        d_all_values[piece_start : piece_start + row_count].astype(jnp.bfloat16), "seq", -offset
    ).astype(jnp.float32)
    own_dkeys = own_dkeys + back_keys
    own_dvalues = own_dvalues + back_values
    d_qkv = jnp.concatenate(
        [
            d_query.reshape(row_count, features),
            own_dkeys.reshape(row_count, features),
            own_dvalues.reshape(row_count, features),
        ],
        1,
    ).astype(jnp.bfloat16)
    grad_qkv = dot_float(low_one.T, d_qkv)
    unused_one, norm_back_one = jax.vjp(layer_norm, inputs, bnorms[6], bnorms[7])
    d_one, grad_gain_one, grad_bias_one = norm_back_one(dot_float(d_qkv, back_qkv.T))
    d_inputs = d_after_self + d_one
    grad_norms = jnp.stack(
        [
            grad_gain_bn1,
            grad_bias_bn1,
            grad_gain_bn2,
            grad_bias_bn2,
            grad_gain_bn3,
            grad_bias_bn3,
            grad_gain_one,
            grad_bias_one,
            grad_gain_two,
            grad_bias_two,
            grad_gain_three,
            grad_bias_three,
        ]
    )
    shard_sums = (
        lax.psum_scatter(grad_patch, "dp", scatter_dimension=0, tiled=True),
        lax.psum_scatter(grad_conv, "dp", scatter_dimension=1, tiled=True),
        lax.psum_scatter(grad_qkv, "dp", scatter_dimension=0, tiled=True),
        lax.psum_scatter(grad_sout, "dp", scatter_dimension=0, tiled=True),
        lax.psum_scatter(grad_cq, "dp", scatter_dimension=0, tiled=True),
        lax.psum_scatter(grad_ckv, "dp", scatter_dimension=0, tiled=True),
        lax.psum_scatter(grad_cout, "dp", scatter_dimension=0, tiled=True),
        lax.psum_scatter(grad_up, "dp", scatter_dimension=0, tiled=True),
        lax.psum_scatter(grad_down, "dp", scatter_dimension=0, tiled=True),
        lax.psum_scatter(grad_norms, "dp", scatter_dimension=1, tiled=True),
    )
    totals = (
        lax.psum(shard_sums[0].astype(jnp.bfloat16), "seq").astype(jnp.float32),
        lax.psum(shard_sums[1].astype(jnp.bfloat16), "seq").astype(jnp.float32),
        lax.psum(shard_sums[2].astype(jnp.bfloat16), "seq").astype(jnp.float32),
        lax.psum(shard_sums[3].astype(jnp.bfloat16), "seq").astype(jnp.float32),
        lax.psum(shard_sums[4].astype(jnp.bfloat16), "seq").astype(jnp.float32),
        lax.psum(shard_sums[5].astype(jnp.bfloat16), "seq").astype(jnp.float32),
        lax.psum(shard_sums[6].astype(jnp.bfloat16), "seq").astype(jnp.float32),
        lax.psum(shard_sums[7].astype(jnp.bfloat16), "seq").astype(jnp.float32),
        lax.psum(shard_sums[8].astype(jnp.bfloat16), "seq").astype(jnp.float32),
        lax.psum(shard_sums[9].astype(jnp.bfloat16), "seq").astype(jnp.float32),
    )
    return (
        result[None].astype(jnp.bfloat16),
        d_inputs[None].astype(jnp.bfloat16),
        prefix_back[None].astype(jnp.bfloat16),
        totals[0],
        totals[1],
        totals[2],
        totals[3],
        totals[4],
        totals[5],
        totals[6],
        totals[7],
        totals[8],
        totals[9],
    )


def solution(mesh):
    return jax.shard_map(
        on_device,
        mesh=mesh,
        in_specs=(
            P("dp", "seq", None),
            P("dp", "seq", None),
            P("dp", "seq", None),
            P("dp"),
            P("dp"),
            P("dp", "seq", None),
            P("dp", None),
            P(None, "dp", None),
            P("dp", None),
            P("dp", None),
            P("dp", None),
            P("dp", None),
            P("dp", None),
            P("dp", None),
            P("dp", None),
            P(None, "dp"),
        ),
        out_specs=(
            P("dp", "seq", None),
            P("dp", "seq", None),
            P("dp", "seq", None),
            P("dp", None),
            P(None, "dp", None),
            P("dp", None),
            P("dp", None),
            P("dp", None),
            P("dp", None),
            P("dp", None),
            P("dp", None),
            P("dp", None),
            P(None, "dp"),
        ),
        check_vma=False,
    )
```

profile of v0, /device:TPU:0, one launch (start us, length us, event | category | flops | bytes accessed | tf_op | source)
XLA Modules:
  0.0 1797.5 jit_solution(15318604324969206957)
XLA Ops:
  13.4 23.5 %all-gather = bf16[16,48,12]{1,2,0:T(8,128)(2,1)S(1)} all-gather(bf16[1,48,12]{1,2,0:T(8,128)(2,1)} %bitcast.416), channel_id=1, replica_groups=mesh['dp'=16,'seq'=2] {'dp'}, dimensions={0}, use_global_device_ids=true | all-gather | bytes 19584 | tf_op jit(solution)/shard_map/all_gather | solution.py:221
  40.7 10.7 all-gather.18.cloned.1.call-done
  53.0 39.7 %all-reduce.26 = (f32[768]{0:T(1024)S(1)}, f32[768]{0:T(1024)S(1)}) all-reduce(f32[768]{0:T(1024)S(1)} %get-tuple-element.254, f32[768]{0:T(1024)S(1)} %get-tuple-element.253), channel_id=1, replica_groups=mesh['dp'=16,'seq'=2] {'dp','seq'}, use_global_device_ids=true, to_apply=%region_7.8 | all-reduce | flops 1536 | bytes 12288 | tf_op jit(solution)/shard_map/psum | solution.py:49
  118.8 25.4 %all-gather.16.cloned.1.call-done = bf16[768,1536]{1,0:T(8,128)(2,1)} async-done(((bf16[48,1536]{1,0:T(8,128)(2,1)}), bf16[768,1536]{1,0:T(8,128)(2,1)}) %all-gather.16.cloned.1.call-update) | async-done | bytes 2359312 | tf_op jit(solution)/shard_map/all_gather | solution.py:217
  159.4 12.1 fusion.6
  171.5 11.9 fusion
  184.4 13.1 fusion.40
  200.3 93.6 %all-gather.20.cloned.1.call-done = bf16[2,6912,768]{2,1,0:T(8,128)(2,1)} async-done(((bf16[2,432,768]{2,1,0:T(8,128)(2,1)}), bf16[2,6912,768]{2,1,0:T(8,128)(2,1)}) %all-gather.20.cloned.1.call-update) | async-done | bytes 21233680 | tf_op jit(solution)/shard_map/all_gather | solution.py:213
  308.7 40.5 %all-reduce.25 = (f32[768]{0:T(1024)S(1)}, f32[768]{0:T(1024)S(1)}) all-reduce(f32[768]{0:T(1024)S(1)} %get-tuple-element.252, f32[768]{0:T(1024)S(1)} %get-tuple-element.251), channel_id=1, replica_groups=mesh['dp'=16,'seq'=2] {'dp','seq'}, use_global_device_ids=true, to_apply=%region_11.12 | all-reduce | flops 1536 | bytes 12288 | tf_op jit(solution)/shard_map/psum | solution.py:49
  378.0 41.7 %all-reduce.24 = (f32[768]{0:T(1024)S(1)}, f32[768]{0:T(1024)S(1)}) all-reduce(f32[768]{0:T(1024)S(1)} %get-tuple-element.250, f32[768]{0:T(1024)S(1)} %get-tuple-element.249), channel_id=1, replica_groups=mesh['dp'=16,'seq'=2] {'dp','seq'}, use_global_device_ids=true, to_apply=%region_15.16 | all-reduce | flops 1536 | bytes 12288 | tf_op jit(solution)/shard_map/psum | solution.py:49
  421.6 10.0 all-gather.1
  450.1 33.8 %all-gather.28.cloned.1.call-done = bf16[3072,768]{1,0:T(8,128)(2,1)} async-done(((bf16[192,768]{1,0:T(8,128)(2,1)}), bf16[3072,768]{1,0:T(8,128)(2,1)}) %all-gather.28.cloned.1.call-update) | async-done | bytes 4718608 | tf_op jit(solution)/shard_map/all_gather | solution.py:220
  483.9 9.0 fusion.13
  535.7 11.1 all-reduce.31.cloned.1.call-done
  550.5 39.4 %all-reduce.23 = (f32[768]{0:T(1024)S(1)}, f32[768]{0:T(1024)S(1)}) all-reduce(f32[768]{0:T(1024)S(1)} %get-tuple-element.238, f32[768]{0:T(1024)S(1)} %get-tuple-element.245), channel_id=1, replica_groups=mesh['dp'=16,'seq'=2] {'dp','seq'}, use_global_device_ids=true, to_apply=%region_35.36 | all-reduce | flops 1536 | bytes 12288 | tf_op jit(solution)/shard_map/psum | solution.py:61
  618.4 42.2 %all-reduce.22 = (f32[768]{0:T(1024)S(1)}, f32[768]{0:T(1024)S(1)}) all-reduce(f32[768]{0:T(1024)S(1)} %get-tuple-element.240, f32[768]{0:T(1024)S(1)} %get-tuple-element.244), channel_id=1, replica_groups=mesh['dp'=16,'seq'=2] {'dp','seq'}, use_global_device_ids=true, to_apply=%region_39.40 | all-reduce | flops 1536 | bytes 12288 | tf_op jit(solution)/shard_map/psum | solution.py:61
  685.2 41.2 %all-reduce.21 = (f32[768]{0:T(1024)S(1)}, f32[768]{0:T(1024)S(1)}) all-reduce(f32[768]{0:T(1024)S(1)} %get-tuple-element.242, f32[768]{0:T(1024)S(1)} %get-tuple-element.243), channel_id=1, replica_groups=mesh['dp'=16,'seq'=2] {'dp','seq'}, use_global_device_ids=true, to_apply=%region_43.44 | all-reduce | flops 1536 | bytes 12288 | tf_op jit(solution)/shard_map/psum | solution.py:61
  746.4 21.5 %multiply_reduce_fusion = (f32[12,512]{1,0:T(8,128)S(1)}, f32[12,512,1024]{2,1,0:T(8,128)}) fusion(f32[12,512]{1,0:T(8,128)S(1)} %log_add_fusion, f32[12,512,1024]{2,1,0:T(8,128)} %get-tuple-element.340, pred[512,1024]{1,0:T(8,128)(4,1)S(1)} %copy-done.16, bf16[512,12,64]{0,2,1:T(8,128)(2,1)S(1)} %bitcast.397, bf16[512,12,64]{0,2,1:T(8,128)(2,1)S(1)} %bitcast.396, ...), kind=kOutput, calls=%fused_computation.2 | convolution fusion | flops 839903232 | bytes 53264384 | tf_op jit(solution)/shard_map/while/body/eval_jaxpr/qhd,khd->hqk/dot_general | solution.py:132
  767.8 18.0 %multiply_convert_fusion = bf16[12,512,1024]{2,1,0:T(8,128)(2,1)S(1)} fusion(f32[12,512,1024]{2,1,0:T(8,128)} %get-tuple-element.355, f32[12,512]{1,0:T(8,128)S(1)} %get-tuple-element.354, f32[12,512]{1,0:T(8,128)S(1)} %log_add_fusion, f32[12,512,1024]{2,1,0:T(8,128)} %get-tuple-element.340, pred[512,1024]{1,0:T(8,128)(4,1)S(1)} %copy-done.16), kind=kLoop, calls=%fused_computation.1 | loop fusion | flops 37748736 | bytes 63488000 | tf_op jit(solution)/shard_map/while/body/eval_jaxpr/convert_element_type | solution.py:134
  792.8 11.5 fusion.27
  806.0 9.0 multiply_convert_fusion.3
  816.8 12.3 collective-permute-done.7
  837.3 7.4 fusion.212
  844.8 10.2 fusion.145
  877.9 23.3 %pad_maximum_fusion = f32[2,6912,768]{2,1,0:T(8,128)} fusion(f32[1,6912,768]{2,1,0:T(8,128)S(1)} %bitcast.382, f32[1,6912,768]{2,1,0:T(8,128)} %bitcast.383), kind=kLoop, calls=%fused_computation | loop fusion | flops 10616832 | bytes 84934656 | tf_op jit(solution)/shard_map/stack | solution.py:398
  919.0 77.1 %reduce-scatter.23.cloned.1.call-done = f32[48,2304]{1,0:T(8,128)} async-done(((f32[768,2304]{1,0:T(8,128)}), f32[48,2304]{1,0:T(8,128)}) %reduce-scatter.23.cloned.1.call-update) | async-done | bytes 442384 | tf_op jit(solution)/shard_map/reduce_scatter | solution.py:449
  997.9 113.7 %reduce-scatter.31.cloned.1.call-done = f32[48,3072]{1,0:T(8,128)} async-done(((f32[768,3072]{1,0:T(8,128)}), f32[48,3072]{1,0:T(8,128)}) %reduce-scatter.31.cloned.1.call-update) | async-done | bytes 589840 | tf_op jit(solution)/shard_map/reduce_scatter | solution.py:454
  1113.4 113.4 %reduce-scatter.33.cloned.1.call-done = f32[192,768]{1,0:T(8,128)} async-done(((f32[3072,768]{1,0:T(8,128)}), f32[192,768]{1,0:T(8,128)}) %reduce-scatter.33.cloned.1.call-update) | async-done | bytes 589840 | tf_op jit(solution)/shard_map/reduce_scatter | solution.py:455
  1228.6 407.1 %reduce-scatter.21.cloned.1.call-done = f32[2,432,768]{2,1,0:T(8,128)} async-done(((f32[2,6912,768]{2,1,0:T(8,128)}), f32[2,432,768]{2,1,0:T(8,128)}) %reduce-scatter.21.cloned.1.call-update) | async-done | bytes 2654224 | tf_op jit(solution)/shard_map/reduce_scatter | solution.py:448
  1638.7 8.9 fusion.41
  1650.5 44.0 %reduce-scatter.41.cloned.1.call-done = f32[48,12]{1,0:T(8,128)} async-done(((f32[768,12]{1,0:T(8,128)}), f32[48,12]{1,0:T(8,128)}) %reduce-scatter.41.cloned.1.call-update) | async-done | bytes 2320
  1700.9 79.9 %all-reduce.33.cloned.1.call-done = (bf16[48,768]{0,1:T(8,128)(2,1)}, bf16[48,1536]{0,1:T(8,128)(2,1)}, bf16[2,432,768]{2,1,0:T(8,128)(2,1)}, bf16[48,2304]{1,0:...) async-done(((bf16[48,768]{0,1:T(8,128)(2,1)}, ...) | async-done | bytes 2580496 | tf_op jit(solution)/shard_map/psum | solution.py:459
  (600 shorter events, 321.8 us)
Async XLA Ops:
  7.2 44.2 %all-gather.18.cloned.1.call-start = ((), (), s32[]{:S(2)}) async-start(), calls=%async_computation.14 | async-start | bytes 1253376 | tf_op jit(solution)/shard_map/all_gather | solution.py:212
  7.9 95.0 %all-gather.12.cloned.1.call-start = ((), (), s32[]{:S(2)}) async-start(), calls=%async_computation.11 | async-start | bytes 3760128 | tf_op jit(solution)/shard_map/all_gather | solution.py:214
  8.7 135.5 %all-gather.16.cloned.1.call-start = ((), (), s32[]{:S(2)}) async-start(), calls=%async_computation.13 | async-start | bytes 2506752 | tf_op jit(solution)/shard_map/all_gather | solution.py:217
  9.4 188.0 %all-gather.14.cloned.1.call-start = ((), (), s32[]{:S(2)}) async-start(), calls=%async_computation.12 | async-start | bytes 1253376 | tf_op jit(solution)/shard_map/all_gather | solution.py:215
  10.0 283.9 %all-gather.20.cloned.1.call-start = ((), (), s32[]{:S(2)}) async-start(), calls=%async_computation.15 | async-start | bytes 22560768 | tf_op jit(solution)/shard_map/all_gather | solution.py:213
  10.6 345.6 %all-gather.22.cloned.1.call-start = ((), (), s32[]{:S(2)}) async-start(), calls=%async_computation.16 | async-start | bytes 1253376 | tf_op jit(solution)/shard_map/all_gather | solution.py:216
  11.2 428.8 %all-gather.24.cloned.1.call-start = ((), (), s32[]{:S(2)}) async-start(), calls=%async_computation.17 | async-start | bytes 1253376 | tf_op jit(solution)/shard_map/all_gather | solution.py:218
  11.9 430.9 %all-gather.26.cloned.1.call-start = ((), (), s32[]{:S(2)}) async-start(), calls=%async_computation.18 | async-start | bytes 5013504 | tf_op jit(solution)/shard_map/all_gather | solution.py:219
  12.7 471.2 %all-gather.28.cloned.1.call-start = ((), (), s32[]{:S(2)}) async-start(), calls=%async_computation.19 | async-start | bytes 5013504 | tf_op jit(solution)/shard_map/all_gather | solution.py:220
  13.4 533.4 %all-reduce.31.cloned.1.call-start = ((), (), s32[]{:S(2)}) async-start(), calls=%async_computation.31 | async-start | bytes 1572864
  92.9 6.1 collective-permute-start.2
  109.7 49.6 %collective-permute-start.1 = (bf16[512,12,64]{0,2,1:T(8,128)(2,1)}, bf16[512,12,64]{0,2,1:T(8,128)(2,1)}, u32[]{:S(2)}, u32[]{:S(2)}) collective-permute-start(bf16[512,12,64]{0,2,1:T(8,128)(2,1)} %bitcast.7), channel_id=1, source_target_pairs={{0,1},{2,3},{4,5},{6,7},{8,9},{10,11},{12,13},{14,15},{16,17},{18,... | collective-permute-start | bytes 2359304 | tf_op jit(solution)/shard_map/ppermute | solution.py:30
  155.7 27.7 %collective-permute-start = (bf16[512,12,64]{0,2,1:T(8,128)(2,1)}, bf16[512,12,64]{0,2,1:T(8,128)(2,1)S(1)}, u32[]{:S(2)}, u32[]{:S(2)}) collective-permute-start(bf16[512,12,64]{0,2,1:T(8,128)(2,1)} %bitcast.394), channel_id=1, source_target_pairs={{0,1},{2,3},{4,5},{6,7},{8,9},{10,11},{12,13},{14,15},{16,17},{18,... | collective-permute-start | bytes 2359304 | tf_op jit(solution)/shard_map/ppermute | solution.py:30
  350.3 10.7 collective-permute-start.4
  354.5 6.5 collective-permute-start.5
  513.8 220.1 %reduce-scatter.35.cloned.1.call-start = ((), (), s32[]{:S(2)}) async-start(), calls=%async_computation.27 | async-start | bytes 147456
  518.9 391.7 %reduce-scatter.27.cloned.1.call-start = ((), (), s32[]{:S(2)}) async-start(), calls=%async_computation.23 | async-start | bytes 2506752 | tf_op jit(solution)/shard_map/reduce_scatter | solution.py:451
  523.3 388.8 %reduce-scatter.29.cloned.1.call-start = ((), (), s32[]{:S(2)}) async-start(), calls=%async_computation.24 | async-start | bytes 2506752 | tf_op jit(solution)/shard_map/reduce_scatter | solution.py:453
  535.6 378.1 %reduce-scatter.25.cloned.1.call-start = ((), (), s32[]{:S(2)}) async-start(), calls=%async_computation.22 | async-start | bytes 2506752 | tf_op jit(solution)/shard_map/reduce_scatter | solution.py:450
  606.7 8.1 collective-permute-start.8
  610.2 305.1 %reduce-scatter.37.cloned.1.call-start = ((), (), s32[]{:S(2)}) async-start(), calls=%async_computation.28 | async-start | bytes 2506752
  610.3 6.1 collective-permute-start.9
  678.7 6.1 collective-permute-start.11
  731.4 185.7 %reduce-scatter.39.cloned.1.call-start = ((), (), s32[]{:S(2)}) async-start(), calls=%async_computation.29 | async-start | bytes 5013504
  744.8 251.4 %reduce-scatter.23.cloned.1.call-start = ((), (), s32[]{:S(2)}) async-start(), calls=%async_computation.21 | async-start | bytes 7520256 | tf_op jit(solution)/shard_map/reduce_scatter | solution.py:449
  791.5 23.6 %collective-permute-start.6 = (bf16[512,12,64]{0,2,1:T(8,128)(2,1)}, bf16[512,12,64]{0,2,1:T(8,128)(2,1)}, u32[]{:S(2)}, u32[]{:S(2)}) collective-permute-start(bf16[512,12,64]{0,2,1:T(8,128)(2,1)} %slice.786), channel_id=1, source_target_pairs={{1,0},{3,2},{5,4},{7,6},{9,8},{11,10},{13,12},{15,14},{17,16},{19,... | collective-permute-start | bytes 2359304 | tf_op jit(solution)/shard_map/ppermute | solution.py:30
  804.4 24.6 %collective-permute-start.7 = (bf16[512,12,64]{0,2,1:T(8,128)(2,1)S(1)}, bf16[512,12,64]{0,2,1:T(8,128)(2,1)}, u32[]{:S(2)}, u32[]{:S(2)}) collective-permute-start(bf16[512,12,64]{0,2,1:T(8,128)(2,1)S(1)} %slice.785), channel_id=1, source_target_pairs={{1,0},{3,2},{5,4},{7,6},{9,8},{11,10},{13,12},{15,14},{17,16},{19,... | collective-permute-start | bytes 2359304 | tf_op jit(solution)/shard_map/ppermute | solution.py:30
  835.9 275.7 %reduce-scatter.31.cloned.1.call-start = ((), (), s32[]{:S(2)}) async-start(), calls=%async_computation.25 | async-start | bytes 10027008 | tf_op jit(solution)/shard_map/reduce_scatter | solution.py:454
  844.8 382.0 %reduce-scatter.33.cloned.1.call-start = ((), (), s32[]{:S(2)}) async-start(), calls=%async_computation.26 | async-start | bytes 10027008 | tf_op jit(solution)/shard_map/reduce_scatter | solution.py:455
  855.1 780.6 %reduce-scatter.21.cloned.1.call-start = ((), (), s32[]{:S(2)}) async-start(), calls=%async_computation.20 | async-start | bytes 45121536 | tf_op jit(solution)/shard_map/reduce_scatter | solution.py:448
  901.3 793.2 %reduce-scatter.41.cloned.1.call-start = ((), (), s32[]{:S(2)}) async-start(), calls=%async_computation.30 | async-start | bytes 417792
  910.2 870.5 %all-reduce.33.cloned.1.call-start = ((), (), s32[]{:S(2)}) async-start(), calls=%async_computation.32 | async-start | bytes 5898240 | tf_op jit(solution)/shard_map/psum | solution.py:459
  (146 other events, 3457.2 us)
Sparse Core Ops, SparseCore 0:
  10.3 41.0 all-gather.17
  53.7 46.8 all-gather.11
  102.8 41.3 all-gather.15
  146.3 37.0 all-gather.13
  184.9 108.9 all-gather.19
  296.1 38.5 all-gather.21
  337.0 37.2 all-gather.23
  376.6 53.2 all-gather.25
  432.1 51.7 all-gather.27
  513.9 32.8 all-reduce.30
  549.6 10.0 reduce-scatter.34
  563.8 62.8 reduce-scatter.26
  630.5 61.9 reduce-scatter.28
  696.6 62.0 reduce-scatter.24
  762.3 62.0 reduce-scatter.36
  828.6 74.6 reduce-scatter.38
  907.1 88.9 reduce-scatter.22
  1000.6 110.8 reduce-scatter.30
  1115.7 111.0 reduce-scatter.32
  1231.5 404.1 reduce-scatter.20
  1639.8 54.7 reduce-scatter.40
  1698.8 81.9 all-reduce.32
where the time goes:
time: 1810 us; the launch traced here: 1800 us
  waiting for transfers between devices  1030 us (57%)
  blocking collectives  288 us (16%)
  matrix products  267 us (15%)
  other arithmetic  97.1 us (5%)
  local copies, waits for them, and re-layouts  57.2 us (3%)
  starting transfers between devices  33.9 us (2%)
  between operations  19.4 us (1%)
    reduce_scatter x1, waiting for transfers between devices, on_device(): lax.psum_scatter(grad_conv, 'dp', scatter_dimension=1, tiled=True)  407 us
    dot_general x80, matrix products, dot_float(): return jnp.dot(left, right, preferred_element_type=jnp.float32)  184 us
    psum x3, blocking collectives, batch_back(): lax.psum((jnp.sum(d_normed, 0), jnp.sum(d_normed * normed, 0)), ('dp', 's...  123 us
    psum x3, blocking collectives, norm_batch(): lax.psum((jnp.sum(values, 0), jnp.sum(values * values, 0)), ('dp', 'seq'))  122 us
    reduce_scatter x1, waiting for transfers between devices, on_device(): lax.psum_scatter(grad_up, 'dp', scatter_dimension=0, tiled=True)  114 us
    reduce_scatter x1, waiting for transfers between devices, on_device(): lax.psum_scatter(grad_down, 'dp', scatter_dimension=0, tiled=True)  113 us
    all_gather x1, waiting for transfers between devices, on_device(): lax.all_gather(w_conv, 'dp', axis=1, tiled=True)  93.6 us
    psum x1, waiting for transfers between devices, on_device(): lax.psum(shard_sums[0].astype(jnp.bfloat16), 'seq').astype(jnp.float32)  79.9 us
  transfers between devices with their start and end apart: 34, of which 15 were waited for; matrix products, arithmetic and copies ran while one was open for 21% of the time, Pallas kernels for 0%

commit v1 on v0

--- a/solution.py
+++ b/solution.py
@@ -1,10 +1,628 @@
+import functools
+
 import jax
 import jax.numpy as jnp
+import numpy as np
 from jax import lax
+from jax.experimental import pallas as pl
+from jax.experimental.pallas import tpu as pltpu
 from jax.sharding import PartitionSpec as P
 
 HEADS = 12
 SIDE = 14
+MESH = pl.DeviceIdType.MESH
+LOW = jnp.bfloat16
+
+STEPS = ((4, 3, 2, 0), (4, 0, 3, 2), (4, 2, 0, 3))
+PORTIONS = 3
+GROUP = 8
+
+
+def my_bits():
+    a = lax.axis_index("dp")
+    return [
+        lax.axis_index("seq"),
+        lax.rem(a, 2),
+        lax.rem(a // 2, 2),
+        lax.rem(a // 4, 2),
+        lax.rem(a // 8, 2),
+    ]
+
+
+def flipped(bits, which):
+    return [1 - b if i == which else b for i, b in enumerate(bits)]
+
+
+def place(bits):
+    return (bits[1] + 2 * bits[2] + 4 * bits[3] + 8 * bits[4], bits[0])
+
+
+def slot_of(bits, p):
+    order = STEPS[p]
+    return (
+        bits[order[0]] + 2 * bits[order[1]] + 4 * bits[order[2]] + 8 * bits[order[3]] + 16 * bits[1]
+    )
+
+
+def device_of_slot(p):
+    owners = np.zeros(32, np.int64)
+    for e in range(32):
+        bits = [(e >> i) & 1 for i in range(5)]
+        owners[int(slot_of(bits, p))] = e
+    return owners
+
+
+def slots_to_devices(array):
+    parts = []
+    for p in range(PORTIONS):
+        rest = array.shape[2:]
+        names = [1, STEPS[p][3], STEPS[p][2], STEPS[p][1], STEPS[p][0]]
+        cube = array[p].reshape((2,) * 5 + rest)
+        perm = [names.index(bit) for bit in (4, 3, 2, 1, 0)]
+        cube = cube.transpose(perm + [5 + i for i in range(len(rest))])
+        parts.append(cube.reshape((32,) + rest))
+    return jnp.stack(parts, 1)
+
+
+def devices_to_slots(array):
+    parts = []
+    for p in range(PORTIONS):
+        rest = array.shape[2:]
+        names = [4, 3, 2, 1, 0]
+        cube = array[:, p].reshape((2,) * 5 + rest)
+        want = [1, STEPS[p][3], STEPS[p][2], STEPS[p][1], STEPS[p][0]]
+        perm = [names.index(bit) for bit in want]
+        cube = cube.transpose(perm + [5 + i for i in range(len(rest))])
+        parts.append(cube.reshape((32,) + rest))
+    return jnp.stack(parts, 0)
+
+
+def greet(places):
+    barrier = pltpu.get_barrier_semaphore()
+    for where in places:
+        pl.semaphore_signal(barrier, inc=1, device_id=where, device_id_type=MESH)
+    pl.semaphore_wait(barrier, len(places))
+
+
+def arrived(ref, sem):
+    pltpu.make_async_remote_copy(
+        src_ref=ref,
+        dst_ref=ref,
+        send_sem=sem,
+        recv_sem=sem,
+        device_id=(lax.axis_index("dp"), 1 - lax.axis_index("seq")),
+        device_id_type=MESH,
+    ).wait_recv()
+
+
+def gather_body(x_ref, o_ref, send_sem, recv_sem, own_sem):
+    bits = my_bits()
+    greet([place(flipped(bits, b)) for b in range(5)])
+    started = []
+
+    def send(p, src, start, size, to_bit, k):
+        copy = pltpu.make_async_remote_copy(
+            src_ref=src,
+            dst_ref=o_ref.at[p, pl.ds(start, size)],
+            send_sem=send_sem.at[p, k],
+            recv_sem=recv_sem.at[p, k],
+            device_id=place(flipped(bits, to_bit)),
+            device_id_type=MESH,
+        )
+        copy.start()
+        started.append(copy)
+
+    def await_run(p, start, size, k):
+        run = o_ref.at[p, pl.ds(start, size)]
+        arrived(run, recv_sem.at[p, k])
+
+    slots = [slot_of(bits, p) for p in range(PORTIONS)]
+    owns = []
+    for p in range(PORTIONS):
+        own = pltpu.make_async_copy(
+            x_ref.at[pl.ds(p, 1)], o_ref.at[p, pl.ds(slots[p], 1)], own_sem.at[p]
+        )
+        own.start()
+        owns.append(own)
+    for p in range(PORTIONS):
+        send(p, x_ref.at[pl.ds(p, 1)], slots[p], 1, STEPS[p][0], 0)
+    for p in range(PORTIONS):
+        send(p, x_ref.at[pl.ds(p, 1)], slots[p], 1, 1, 4)
+    for own in owns:
+        own.wait()
+    fresh = [None] * PORTIONS
+    for k in range(4):
+        size = 2**k
+        for p in range(PORTIONS):
+            mine = (slots[p] // size) * size
+            bit = bits[STEPS[p][k]]
+            theirs = mine + size * (1 - 2 * bit)
+            await_run(p, theirs, size, k)
+            fresh[p] = theirs
+            if k < 3:
+                both = (slots[p] // (2 * size)) * (2 * size)
+                send(p, o_ref.at[p, pl.ds(both, 2 * size)], both, 2 * size, STEPS[p][k + 1], k + 1)
+        for p in range(PORTIONS):
+            send(p, o_ref.at[p, pl.ds(fresh[p], size)], fresh[p], size, 1, 5 + k)
+    for p in range(PORTIONS):
+        other = 16 * (1 - 2 * bits[1])
+        await_run(p, slots[p] + other, 1, 4)
+        for k in range(4):
+            size = 2**k
+            mine = (slots[p] // size) * size
+            theirs = mine + size * (1 - 2 * bits[STEPS[p][k]])
+            await_run(p, theirs + other, size, 5 + k)
+    for copy in started:
+        copy.wait_send()
+
+
+def gather_all(x, cid):
+    return pl.pallas_call(
+        gather_body,
+        name="gather_all",
+        out_shape=jax.ShapeDtypeStruct((PORTIONS, 32) + x.shape[1:], x.dtype),
+        in_specs=[pl.BlockSpec(memory_space=pltpu.HBM)],
+        out_specs=pl.BlockSpec(memory_space=pltpu.HBM),
+        scratch_shapes=[
+            pltpu.SemaphoreType.DMA((PORTIONS, 9)),
+            pltpu.SemaphoreType.DMA((PORTIONS, 9)),
+            pltpu.SemaphoreType.DMA((PORTIONS,)),
+        ],
+        compiler_params=pltpu.CompilerParams(collective_id=cid, has_side_effects=True),
+    )(x)
+
+
+def reduce_body(x_ref, o_ref, r0, r1, r2, r3, r4, send_sem, recv_sem):
+    bits = my_bits()
+    greet([place(flipped(bits, b)) for b in range(5)])
+    started = []
+    slots = [slot_of(bits, p) for p in range(PORTIONS)]
+    bufs = (r0, r1, r2, r3, r4)
+
+    def send(p, src, dst, bit, k):
+        copy = pltpu.make_async_remote_copy(
+            src_ref=src,
+            dst_ref=dst,
+            send_sem=send_sem.at[p, k],
+            recv_sem=recv_sem.at[p, k],
+            device_id=place(flipped(bits, bit)),
+            device_id_type=MESH,
+        )
+        copy.start()
+        started.append(copy)
+
+    for p in range(PORTIONS):
+        away = 16 * (1 - bits[1])
+        send(p, x_ref.at[p, pl.ds(away, 16)], r0.at[p], 1, 0)
+    for k in range(5):
+        size = 16 >> k
+        for p in range(PORTIONS):
+            got = bufs[k].at[p]
+            arrived(got, recv_sem.at[p, k])
+            if k == 0:
+                base, held = 16 * bits[1], x_ref
+            else:
+                bit = bits[STEPS[p][4 - k]]
+                base, held = size * bit, bufs[k - 1]
+            if k == 4:
+                o_ref[p] = held[p, base].astype(jnp.float32) + bufs[k][p, 0].astype(jnp.float32)
+                continue
+            for j in range(size):
+                total = held[p, base + j].astype(jnp.float32) + bufs[k][p, j].astype(jnp.float32)
+                bufs[k][p, j] = total.astype(bufs[k].dtype)
+            half = size // 2
+            nbit = bits[STEPS[p][3 - k]]
+            send(
+                p,
+                bufs[k].at[p, pl.ds(half * (1 - nbit), half)],
+                bufs[k + 1].at[p],
+                STEPS[p][3 - k],
+                k + 1,
+            )
+    for copy in started:
+        copy.wait_send()
+
+
+def reduce_all(x, cid):
+    rest = x.shape[2:]
+    return pl.pallas_call(
+        reduce_body,
+        name="reduce_all",
+        out_shape=jax.ShapeDtypeStruct((PORTIONS,) + rest, jnp.float32),
+        in_specs=[pl.BlockSpec(memory_space=pltpu.VMEM)],
+        out_specs=pl.BlockSpec(memory_space=pltpu.VMEM),
+        scratch_shapes=[pltpu.VMEM((PORTIONS, 16 >> k) + rest, x.dtype) for k in range(5)]
+        + [pltpu.SemaphoreType.DMA((PORTIONS, 5)), pltpu.SemaphoreType.DMA((PORTIONS, 5))],
+        compiler_params=pltpu.CompilerParams(
+            collective_id=cid, has_side_effects=True, vmem_limit_bytes=40 << 20
+        ),
+    )(x)
+
+
+def swap_body(x_ref, o_ref, send_sem, recv_sem, own_sem):
+    a, s = lax.axis_index("dp"), lax.axis_index("seq")
+    count = x_ref.shape[0]
+    greet([(lax.rem(a + j, count), s) for j in range(1, count)])
+    own = pltpu.make_async_copy(x_ref.at[a], o_ref.at[a], own_sem)
+    own.start()
+    copies = []
+    for j in range(1, count):
+        to = lax.rem(a + j, count)
+        copy = pltpu.make_async_remote_copy(
+            src_ref=x_ref.at[to],
+            dst_ref=o_ref.at[a],
+            send_sem=send_sem.at[j],
+            recv_sem=recv_sem.at[j],
+            device_id=(to, s),
+            device_id_type=MESH,
+        )
+        copy.start()
+        copies.append(copy)
+    for j in range(1, count):
+        got = o_ref.at[lax.rem(a - j + count, count)]
+        arrived(got, recv_sem.at[j])
+    for copy in copies:
+        copy.wait_send()
+    own.wait()
+
+
+def swap_dp(x, cid):
+    count = x.shape[0]
+    return pl.pallas_call(
+        swap_body,
+        name="swap_dp",
+        out_shape=jax.ShapeDtypeStruct(x.shape, x.dtype),
+        in_specs=[pl.BlockSpec(memory_space=pltpu.HBM)],
+        out_specs=pl.BlockSpec(memory_space=pltpu.HBM),
+        scratch_shapes=[
+            pltpu.SemaphoreType.DMA((count,)),
+            pltpu.SemaphoreType.DMA((count,)),
+            pltpu.SemaphoreType.DMA,
+        ],
+        compiler_params=pltpu.CompilerParams(collective_id=cid, has_side_effects=True),
+    )(x)
+
+
+def swap_both_body(x_ref, o_ref, send_sem, recv_sem, pass_sem, got_sem, own_sem):
+    a, s = lax.axis_index("dp"), lax.axis_index("seq")
+    count = x_ref.shape[0]
+    greet([(lax.rem(a + j, count), s) for j in range(1, count)] + [(a, 1 - s)])
+    own = pltpu.make_async_copy(x_ref.at[a], o_ref.at[s, a], own_sem)
+    own.start()
+    copies = []
+
+    def pass_on(src, slot, j):
+        copy = pltpu.make_async_remote_copy(
+            src_ref=src,
+            dst_ref=o_ref.at[s, slot],
+            send_sem=pass_sem.at[j],
+            recv_sem=got_sem.at[j],
+            device_id=(a, 1 - s),
+            device_id_type=MESH,
+        )
+        copy.start()
+        copies.append(copy)
+
+    pass_on(x_ref.at[a], a, 0)
+    for j in range(1, count):
+        to = lax.rem(a + j, count)
+        copy = pltpu.make_async_remote_copy(
+            src_ref=x_ref.at[to],
+            dst_ref=o_ref.at[s, a],
+            send_sem=send_sem.at[j],
+            recv_sem=recv_sem.at[j],
+            device_id=(to, s),
+            device_id_type=MESH,
+        )
+        copy.start()
+        copies.append(copy)
+    for j in range(1, count):
+        source = lax.rem(a - j + count, count)
+        got = o_ref.at[s, source]
+        arrived(got, recv_sem.at[j])
+        pass_on(got, source, j)
+    for j in range(count):
+        got = o_ref.at[1 - s, lax.rem(a - j + count, count)]
+        arrived(got, got_sem.at[j])
+    for copy in copies:
+        copy.wait_send()
+    own.wait()
+
+
+def swap_both(x, cid):
+    count = x.shape[0]
+    return pl.pallas_call(
+        swap_both_body,
+        name="swap_both",
+        out_shape=jax.ShapeDtypeStruct((2,) + x.shape, x.dtype),
+        in_specs=[pl.BlockSpec(memory_space=pltpu.HBM)],
+        out_specs=pl.BlockSpec(memory_space=pltpu.HBM),
+        scratch_shapes=[pltpu.SemaphoreType.DMA((count,))] * 4 + [pltpu.SemaphoreType.DMA],
+        compiler_params=pltpu.CompilerParams(collective_id=cid, has_side_effects=True),
+    )(x)
+
+
+def exchange_body(x_ref, o_ref, send_sem, recv_sem, own_sem):
+    e = 2 * lax.axis_index("dp") + lax.axis_index("seq")
+    count = x_ref.shape[0]
+
+    def where(number):
+        return (number // 2, lax.rem(number, 2))
+
+    greet([where(lax.rem(e + j, count)) for j in range(1, count)])
+    own = pltpu.make_async_copy(x_ref.at[e], o_ref.at[e], own_sem)
+    own.start()
+    copies = []
+    for j in range(1, count):
+        to = lax.rem(e + j, count)
+        copy = pltpu.make_async_remote_copy(
+            src_ref=x_ref.at[to],
+            dst_ref=o_ref.at[e],
+            send_sem=send_sem.at[j],
+            recv_sem=recv_sem.at[j],
+            device_id=where(to),
+            device_id_type=MESH,
+        )
+        copy.start()
+        copies.append(copy)
+    for j in range(1, count):
+        got = o_ref.at[lax.rem(e - j + count, count)]
+        arrived(got, recv_sem.at[j])
+    for copy in copies:
+        copy.wait_send()
+    own.wait()
+
+
+def exchange_all(x, cid):
+    count = x.shape[0]
+    return pl.pallas_call(
+        exchange_body,
+        name="exchange_all",
+        out_shape=jax.ShapeDtypeStruct(x.shape, x.dtype),
+        in_specs=[pl.BlockSpec(memory_space=pltpu.HBM)],
+        out_specs=pl.BlockSpec(memory_space=pltpu.HBM),
+        scratch_shapes=[
+            pltpu.SemaphoreType.DMA((count,)),
+            pltpu.SemaphoreType.DMA((count,)),
+            pltpu.SemaphoreType.DMA,
+        ],
+        compiler_params=pltpu.CompilerParams(collective_id=cid, has_side_effects=True),
+    )(x)
+
+
+def pair_body(x_ref, o_ref, send_sem, recv_sem):
+    a, s = lax.axis_index("dp"), lax.axis_index("seq")
+    greet([(a, 1 - s)])
+    copy = pltpu.make_async_remote_copy(
+        src_ref=x_ref,
+        dst_ref=o_ref,
+        send_sem=send_sem,
+        recv_sem=recv_sem,
+        device_id=(a, 1 - s),
+        device_id_type=MESH,
+    )
+    copy.start()
+    copy.wait()
+
+
+def pair_swap(x, cid):
+    return pl.pallas_call(
+        pair_body,
+        name="pair_swap",
+        out_shape=jax.ShapeDtypeStruct(x.shape, x.dtype),
+        in_specs=[pl.BlockSpec(memory_space=pltpu.HBM)],
+        out_specs=pl.BlockSpec(memory_space=pltpu.HBM),
+        scratch_shapes=[pltpu.SemaphoreType.DMA, pltpu.SemaphoreType.DMA],
+        compiler_params=pltpu.CompilerParams(collective_id=cid, has_side_effects=True),
+    )(x)
+
+
+GELU_C = 0.7978845608028654
+GELU_A = 0.044715
+
+
+def gelu_of(x):
+    return 0.5 * x * (1.0 + jnp.tanh(GELU_C * (x + GELU_A * (x * x * x))))
+
+
+def gelu_slope(x):
+    t = jnp.tanh(GELU_C * (x + GELU_A * (x * x * x)))
+    return 0.5 * (1.0 + t) + 0.5 * x * (1.0 - t * t) * (GELU_C * (1.0 + 3.0 * GELU_A * (x * x)))
+
+
+CHUNK = 640
+
+
+def tap_masks(cells, examples):
+    rows = examples * SIDE * SIDE
+    at = np.arange(rows)
+    i, j = (at // SIDE) % SIDE, at % SIDE
+    out = np.zeros((16, cells), np.float32)
+    for r in range(3):
+        for c in range(3):
+            ok = (i + r - 1 >= 0) & (i + r - 1 < SIDE) & (j + c - 1 >= 0) & (j + c - 1 < SIDE)
+            out[3 * r + c, :rows] = ok
+    out[9, :rows] = 1.0
+    return out
+
+
+def tap_shift(tap):
+    return SIDE * (tap // 3 - 1) + tap % 3 - 1
+
+
+def norm_act(values, valid, gain, bias, number):
+    centre = jnp.sum(values, 1, keepdims=True) / number
+    away = jnp.where(valid > 0, values - centre, 0.0)
+    rstd = lax.rsqrt(jnp.sum(away * away, 1, keepdims=True) / number + 1e-05)
+    normed = away * rstd
+    return normed, rstd, gelu_of(normed * gain + bias)
+
+
+def put_low(x_ref, y):
+    for p in range(PORTIONS):
+        x_ref[p] = y[GROUP * p : GROUP * (p + 1)].astype(x_ref.dtype)
+
+
+def first_body(number, p_ref, w_ref, gb_ref, m_ref, n_ref, rstd_ref, y_ref, x_ref, v_ref):
+    cells = p_ref.shape[0]
+    for start in range(0, cells, CHUNK):
+        v_ref[:, start : start + CHUNK] = lax.dot_general(
+            w_ref[...],
+            p_ref[start : start + CHUNK, :],
+            (((1,), (1,)), ((), ())),
+            preferred_element_type=jnp.float32,
+        )
+    normed, rstd, act = norm_act(v_ref[...], m_ref[9:10, :], gb_ref[:, 0:1], gb_ref[:, 1:2], number)
+    n_ref[...] = normed
+    rstd_ref[...] = jnp.broadcast_to(rstd, rstd_ref.shape)
+    y_ref[...] = act
+    put_low(x_ref, act)
+
+
+def conv_body(number, layer, x_in, w_ref, gb_ref, m_ref, y_in, n_ref, rstd_ref, y_ref, x_ref, z_ref):
+    cells = x_in.shape[1]
+    rows = y_in.shape[0]
+    for start in range(0, cells, CHUNK):
+        z_ref[:, start : start + CHUNK] = jnp.dot(
+            w_ref[...], x_in[:, start : start + CHUNK], preferred_element_type=jnp.float32
+        )
+    total = jnp.zeros((rows, cells), jnp.float32)
+    for tap in range(9):
+        moved = z_ref[rows * tap : rows * (tap + 1), :]
+        shift = (-tap_shift(tap)) % cells
+        if shift:
+            moved = pltpu.roll(moved, shift, 1)
+        total = total + jnp.where(m_ref[tap : tap + 1, :] > 0, moved, 0.0)
+    normed, rstd, act = norm_act(
+        total,
+        m_ref[9:10, :],
+        gb_ref[:, 2 * layer : 2 * layer + 1],
+        gb_ref[:, 2 * layer + 1 : 2 * layer + 2],
+        number,
+    )
+    n_ref[...] = normed
+    rstd_ref[...] = jnp.broadcast_to(rstd, rstd_ref.shape)
+    y = y_in[...] + act
+    y_ref[...] = y
+    put_low(x_ref, y)
+
+
+def norm_slope(number, dy, normed, rstd, gain, bias):
+    e = dy * gelu_slope(normed * gain + bias)
+    d_gain = jnp.sum(e * normed, 1, keepdims=True)
+    d_bias = jnp.sum(e, 1, keepdims=True)
+    dn = e * gain
+    mean_dn = d_bias * gain / number
+    mean_dnn = d_gain * gain / number
+    return rstd * (dn - mean_dn - normed * mean_dnn), d_gain, d_bias
+
+
+def conv_back_body(
+    number, layer, dy_ref, n_ref, rstd_ref, gb_ref, m_ref, x_in, wt_ref, dx_ref, g_ref, s_ref, d_ref
+):
+    cells = x_in.shape[1]
+    rows = dy_ref.shape[0]
+    dv, d_gain, d_bias = norm_slope(
+        number,
+        dy_ref[...],
+        n_ref[...],
+        rstd_ref[:, 0:1],
+        gb_ref[:, 2 * layer : 2 * layer + 1],
+        gb_ref[:, 2 * layer + 1 : 2 * layer + 2],
+    )
+    lanes = lax.broadcasted_iota(jnp.int32, s_ref.shape, 1)
+    s_ref[...] = jnp.where(lanes == 0, d_gain, d_bias)
+    for tap in range(9):
+        shift = tap_shift(tap) % cells
+        moved = pltpu.roll(dv, shift, 1) if shift else dv
+        moved = jnp.where(m_ref[8 - tap : 9 - tap, :] > 0, moved, 0.0)
+        d_ref[rows * tap : rows * (tap + 1), :] = moved.astype(d_ref.dtype)
+    for start in range(0, cells, CHUNK):
+        dx_ref[:, start : start + CHUNK] = jnp.dot(
+            wt_ref[...], d_ref[:, start : start + CHUNK], preferred_element_type=jnp.float32
+        ).astype(dx_ref.dtype)
+    for start in range(0, x_in.shape[0], 256):
+        g_ref[:, start : start + 256] = lax.dot_general(
+            d_ref[...],
+            x_in[start : start + 256, :],
+            (((1,), (1,)), ((), ())),
+            preferred_element_type=jnp.float32,
+        ).astype(g_ref.dtype)
+
+
+def first_back_body(number, dy_ref, n_ref, rstd_ref, gb_ref, p_ref, g_ref, s_ref):
+    dv, d_gain, d_bias = norm_slope(
+        number, dy_ref[...], n_ref[...], rstd_ref[:, 0:1], gb_ref[:, 0:1], gb_ref[:, 1:2]
+    )
+    lanes = lax.broadcasted_iota(jnp.int32, s_ref.shape, 1)
+    s_ref[...] = jnp.where(lanes == 0, d_gain, d_bias)
+    g_ref[...] = jnp.dot(
+        dv.astype(p_ref.dtype), p_ref[...], preferred_element_type=jnp.float32
+    ).astype(g_ref.dtype)
+
+
+BIG = pltpu.CompilerParams(vmem_limit_bytes=48 << 20)
+
+
+def first_block(pixels, w, gb, masks, number):
+    rows, cells = w.shape[0], pixels.shape[0]
+    return pl.pallas_call(
+        functools.partial(first_body, number),
+        name="stem_first",
+        out_shape=(
+            jax.ShapeDtypeStruct((rows, cells), jnp.float32),
+            jax.ShapeDtypeStruct((rows, 128), jnp.float32),
+            jax.ShapeDtypeStruct((rows, cells), jnp.float32),
+            jax.ShapeDtypeStruct((PORTIONS, GROUP, cells), LOW),
+        ),
+        scratch_shapes=[pltpu.VMEM((rows, cells), jnp.float32)],
+        compiler_params=BIG,
+    )(pixels, w, gb, masks)
+
+
+def conv_block(layer, x_all, w, gb, masks, y, number):
+    rows, cells = y.shape
+    return pl.pallas_call(
+        functools.partial(conv_body, number, layer),
+        name="stem_conv",
+        out_shape=(
+            jax.ShapeDtypeStruct((rows, cells), jnp.float32),
+            jax.ShapeDtypeStruct((rows, 128), jnp.float32),
+            jax.ShapeDtypeStruct((rows, cells), jnp.float32),
+            jax.ShapeDtypeStruct((PORTIONS, GROUP, cells), LOW),
+        ),
+        scratch_shapes=[pltpu.VMEM((9 * rows, cells), jnp.float32)],
+        compiler_params=BIG,
+    )(x_all, w, gb, masks, y)
+
+
+def conv_block_back(layer, dy, normed, rstd, gb, masks, x_all, w_t, number):
+    rows, cells = dy.shape
+    features = x_all.shape[0]
+    return pl.pallas_call(
+        functools.partial(conv_back_body, number, layer),
+        name="stem_conv_back",
+        out_shape=(
+            jax.ShapeDtypeStruct((features, cells), LOW),
+            jax.ShapeDtypeStruct((9 * rows, features), LOW),
+            jax.ShapeDtypeStruct((rows, 128), jnp.float32),
+        ),
+        scratch_shapes=[pltpu.VMEM((9 * rows, cells), LOW)],
+        compiler_params=BIG,
+    )(dy, normed, rstd, gb, masks, x_all, w_t)
+
+
+def first_block_back(dy, normed, rstd, gb, pixels, number):
+    rows, cells = dy.shape
+    return pl.pallas_call(
+        functools.partial(first_back_body, number),
+        name="stem_first_back",
+        out_shape=(
+            jax.ShapeDtypeStruct((rows, pixels.shape[1]), LOW),
+            jax.ShapeDtypeStruct((rows, 128), jnp.float32),
+        ),
+        compiler_params=BIG,
+    )(dy, normed, rstd, gb, pixels)
 
 
 def padded_2(cells, sides, width):
@@ -190,7 +808,7 @@
     return (d_query.reshape(queries.shape), sums_kv[0], sums_kv[1])
 
 
-def on_device(
+def general_device(
     captions,
     patches,
     prefix,
@@ -484,9 +1102,333 @@
     )
 
 
+def low_dot(left, right):
+    return dot_float(left, right).astype(LOW)
+
+
+def dot_t(left, right):
+    return lax.dot_general(left, right, (((1,), (1,)), ((), ())), preferred_element_type=jnp.float32)
+
+
+def t_dot(left, right):
+    return lax.dot_general(left, right, (((0,), (0,)), ((), ())), preferred_element_type=jnp.float32)
+
+
+def stem_weights(w_patch, w_conv, norm_params, s):
+    depth, conv_rows, patch_rows = w_conv.shape[0], w_conv.shape[1], w_patch.shape[0]
+    features = w_patch.shape[1]
+    flat = jnp.concatenate([w_conv.reshape(-1, features), w_patch], 0).T
+    blocks = slots_to_devices(flat.reshape(PORTIONS, 32, GROUP, flat.shape[1]))
+    blocks = blocks.reshape(16, 2, PORTIONS * GROUP, flat.shape[1])
+    blocks = lax.dynamic_index_in_dim(blocks, s, 1, keepdims=False)
+    rows = PORTIONS * GROUP
+    extra = jnp.pad(norm_params, ((0, rows - norm_params.shape[0]), (0, 0)))
+    blocks = jnp.concatenate([blocks, jnp.broadcast_to(extra, (16,) + extra.shape)], 2)
+    got = swap_dp(blocks, 0)
+    convs = []
+    for layer in range(depth):
+        part = got[:, :, layer * conv_rows : (layer + 1) * conv_rows]
+        part = part.transpose(1, 0, 2).reshape(rows, 9, features).transpose(1, 0, 2)
+        convs.append(part.reshape(9 * rows, features))
+    at = depth * conv_rows
+    patch = got[:, :, at : at + patch_rows].transpose(1, 0, 2).reshape(rows, -1)
+    at = at + patch_rows
+    norms = got[:, : norm_params.shape[0], at:].transpose(1, 0, 2).reshape(norm_params.shape[0], -1)
+    return convs, patch, norms
+
+
+def own_columns(norms):
+    bits = my_bits()
+    cut = norms.reshape(norms.shape[0], PORTIONS, 32, GROUP)
+    parts = [
+        lax.dynamic_index_in_dim(cut[:, p], slot_of(bits, p), 1, keepdims=False)
+        for p in range(PORTIONS)
+    ]
+    mine = jnp.concatenate(parts, 1).T
+    return jnp.pad(mine, ((0, 0), (0, 128 - mine.shape[1])))
+
+
+def fast_device(
+    captions,
+    patches,
+    prefix,
+    prefix_count,
+    caption_len,
+    cotangent,
+    w_patch,
+    w_conv,
+    w_self_qkv,
+    w_self_out,
+    w_cross_q,
+    w_cross_kv,
+    w_cross_out,
+    w_up,
+    w_down,
+    norm_params,
+):
+    a_index, s_index = lax.axis_index("dp"), lax.axis_index("seq")
+    examples, halves = 16, 2
+    features = w_self_out.shape[1]
+    score_scale = (features // HEADS) ** (-0.5)
+
+    def chunks(w):
+        return [w[:, i * features : (i + 1) * features] for i in range(w.shape[1] // features)]
+
+    qkv_w = lax.all_gather(jnp.stack(chunks(w_self_qkv)), "dp", axis=1, tiled=True)
+    rest_w = lax.all_gather(
+        jnp.stack([w_self_out, w_cross_q] + chunks(w_cross_kv) + [w_cross_out] + chunks(w_up)),
+        "dp",
+        axis=1,
+        tiled=True,
+    )
+    down_w = lax.all_gather(w_down, "dp", axis=0, tiled=True)
+    sout_w, cq_w, ck_w, cv_w, cout_w = (rest_w[i] for i in range(5))
+    up_ws = [rest_w[5 + i] for i in range(4)]
+    down_ws = [down_w[i * features : (i + 1) * features] for i in range(4)]
+
+    convs, patch_w, norms_low = stem_weights(w_patch, w_conv, norm_params, s_index)
+    norms = norms_low.astype(jnp.float32)
+    own_gb = own_columns(norms[:6])
+    own_cells = patches.shape[1]
+    number = own_cells * examples * halves
+    cells = -(-number // CHUNK) * CHUNK
+    masks = jnp.asarray(tap_masks(cells, examples))
+    pixels_split = patches[0].reshape(own_cells, PORTIONS, -1).transpose(1, 0, 2)
+    pixels = slots_to_devices(gather_all(pixels_split, 1))
+    pixels = pixels.transpose(0, 2, 1, 3).reshape(number, -1)
+    pixels = jnp.pad(pixels, ((0, cells - number), (0, 0)))
+    n1, r1, y1, x1 = first_block(pixels, patch_w, own_gb, masks, number)
+    x1_all = gather_all(x1, 2).reshape(features, cells)
+    n2, r2, y2, x2 = conv_block(1, x1_all, convs[0], own_gb, masks, y1, number)
+    x2_all = gather_all(x2, 3).reshape(features, cells)
+    n3, r3, y3, x3 = conv_block(2, x2_all, convs[1], own_gb, masks, y2, number)
+    rows_own = PORTIONS * GROUP
+    grid = halves * own_cells
+    out_blocks = x3.reshape(rows_own, cells)[:, :number].reshape(rows_own, examples, grid)
+    out_blocks = jnp.broadcast_to(
+        out_blocks.transpose(1, 0, 2)[:, None], (examples, halves, rows_own, grid)
+    )
+    in_blocks = exchange_all(out_blocks.reshape(32, rows_own, grid), 4)
+    patch_all = devices_to_slots(in_blocks.reshape(32, PORTIONS, GROUP, grid))
+    patch_all = patch_all.reshape(features, grid).T
+
+    prefix_own = prefix[0]
+    prefix_half = prefix_own.shape[0]
+    prefix_other = lax.ppermute(prefix_own, "seq", [(0, 1), (1, 0)])
+    first_half = s_index == 0
+    prefix_all = jnp.concatenate(
+        [
+            jnp.where(first_half, prefix_own, prefix_other),
+            jnp.where(first_half, prefix_other, prefix_own),
+        ],
+        0,
+    )
+    memory = jnp.concatenate([prefix_all, patch_all], 0)
+    mem_rows = memory.shape[0]
+    prefix_total = prefix_all.shape[0]
+    mem_keys = heads_of(low_dot(memory, ck_w))
+    mem_values = heads_of(low_dot(memory, cv_w))
+    slot_ids = jnp.arange(mem_rows, dtype=jnp.int32)
+    mem_allowed = (slot_ids >= prefix_total) | (slot_ids < prefix_count[0])
+
+    def cross_allow(first_row, block_rows):
+        return jnp.broadcast_to(mem_allowed[None], (block_rows, mem_rows))
+
+    inputs = captions[0].astype(jnp.float32)
+    row_count = inputs.shape[0]
+    low_one = layer_norm(inputs, norms[6], norms[7]).astype(LOW)
+    queries, own_keys, own_values = (heads_of(low_dot(low_one, qkv_w[i])) for i in range(3))
+    got_keys, got_values = passed_along((own_keys, own_values), "seq", 1)
+    all_keys = jnp.concatenate([got_keys, own_keys], 0)
+    all_values = jnp.concatenate([got_values, own_values], 0)
+    ids = jnp.arange(row_count, dtype=jnp.int32)
+    key_pos = jnp.concatenate([(s_index - 1) * row_count + ids, s_index * row_count + ids], 0)
+    length_one = caption_len[0]
+
+    def self_allow(first_row, block_rows):
+        query_pos = s_index * row_count + first_row + jnp.arange(block_rows, dtype=jnp.int32)
+        return (
+            (key_pos[None] <= query_pos[:, None])
+            & (key_pos[None] >= 0)
+            & (key_pos[None] < length_one)
+        )
+
+    self_out, self_total = run_attention(queries, all_keys, all_values, self_allow, score_scale)
+    self_low = self_out.reshape(row_count, features).astype(LOW)
+    after_self = inputs + dot_float(self_low, sout_w)
+    low_two = layer_norm(after_self, norms[8], norms[9]).astype(LOW)
+    cross_q = heads_of(low_dot(low_two, cq_w))
+    cross_out, cross_total = run_attention(cross_q, mem_keys, mem_values, cross_allow, score_scale)
+    cross_low = cross_out.reshape(row_count, features).astype(LOW)
+    after_cross = after_self + dot_float(cross_low, cout_w)
+    low_three = layer_norm(after_cross, norms[10], norms[11]).astype(LOW)
+    ups = [dot_float(low_three, w) for w in up_ws]
+    hiddens = [jax.nn.gelu(u).astype(LOW) for u in ups]
+    result = after_cross
+    for h, w in zip(hiddens, down_ws):
+        result = result + dot_float(h, w)
+
+    out_grad = cotangent[0].astype(jnp.float32)
+    grad_low = cotangent[0]
+    grads_down = low_dot(jnp.concatenate(hiddens, 1).T, grad_low)
+    d_uppers = []
+    for u, w in zip(ups, down_ws):
+        d_uppers.append((dot_t(grad_low, w) * gelu_slope(u)).astype(LOW))
+    grads_up = [t_dot(low_three, d).astype(LOW) for d in d_uppers]
+    d_normed = dot_t(d_uppers[0], up_ws[0])
+    for d, w in zip(d_uppers[1:], up_ws[1:]):
+        d_normed = d_normed + dot_t(d, w)
+    unused_three, norm_back_three = jax.vjp(layer_norm, after_cross, norms[10], norms[11])
+    d_three, grad_gain_three, grad_bias_three = norm_back_three(d_normed)
+    down_parts = grads_down.reshape(examples, 4, -1, features).transpose(1, 0, 2, 3)
+    down_parts = down_parts.reshape(4, features, features)
+    late_sums = [
+        lax.psum_scatter(
+            jnp.concatenate([down_parts, jnp.stack(grads_up)], 0),
+            "dp",
+            scatter_dimension=1,
+            tiled=True,
+        )
+    ]
+    d_after_cross = out_grad + d_three
+    cross_grad_low = d_after_cross.astype(LOW)
+    grad_cout = t_dot(cross_low, cross_grad_low).astype(LOW)
+    d_cross = heads_of(dot_t(cross_grad_low, cout_w).astype(LOW))
+    d_cross_q, d_mem_keys, d_mem_values = run_back(
+        cross_q, mem_keys, mem_values, cross_allow, score_scale, d_cross, cross_total
+    )
+    d_cross_low = d_cross_q.reshape(row_count, features).astype(LOW)
+    grad_cq = t_dot(low_two, d_cross_low).astype(LOW)
+    unused_two, norm_back_two = jax.vjp(layer_norm, after_self, norms[8], norms[9])
+    d_two, grad_gain_two, grad_bias_two = norm_back_two(dot_t(d_cross_low, cq_w))
+    d_after_self = d_after_cross + d_two
+    d_memory = jnp.concatenate(
+        [d_mem_keys.reshape(mem_rows, features), d_mem_values.reshape(mem_rows, features)], 1
+    )
+
+    def half_of(array, which):
+        return jnp.concatenate(
+            [
+                lax.dynamic_slice_in_dim(array, which * prefix_half, prefix_half, 0),
+                lax.dynamic_slice_in_dim(array, prefix_total + which * own_cells, own_cells, 0),
+            ],
+            0,
+        )
+
+    theirs = pair_swap(half_of(d_memory, 1 - s_index).astype(LOW), 5)
+    mine_low = (half_of(d_memory, s_index) + theirs.astype(jnp.float32)).astype(LOW)
+    memory_own = half_of(memory, s_index)
+    grad_ck = t_dot(memory_own, mine_low[:, :features]).astype(LOW)
+    grad_cv = t_dot(memory_own, mine_low[:, features:]).astype(LOW)
+    d_mem_rows = dot_t(mine_low[:, :features], ck_w) + dot_t(mine_low[:, features:], cv_w)
+    prefix_back = d_mem_rows[:prefix_half]
+    d_third = d_mem_rows[prefix_half:].astype(LOW)
+
+    self_grad_low = d_after_self.astype(LOW)
+    grad_sout = t_dot(self_low, self_grad_low).astype(LOW)
+    d_self = heads_of(dot_t(self_grad_low, sout_w).astype(LOW))
+    d_query, d_all_keys, d_all_values = run_back(
+        queries, all_keys, all_values, self_allow, score_scale, d_self, self_total
+    )
+    back_keys, back_values = passed_along(
+        (d_all_keys[:row_count].astype(LOW), d_all_values[:row_count].astype(LOW)), "seq", -1
+    )
+    own_dkeys = d_all_keys[row_count:] + back_keys.astype(jnp.float32)
+    own_dvalues = d_all_values[row_count:] + back_values.astype(jnp.float32)
+    d_qkv = [g.reshape(row_count, features).astype(LOW) for g in (d_query, own_dkeys, own_dvalues)]
+    grads_qkv = [t_dot(low_one, g).astype(LOW) for g in d_qkv]
+    unused_one, norm_back_one = jax.vjp(layer_norm, inputs, norms[6], norms[7])
+    d_normed_one = dot_t(d_qkv[0], qkv_w[0]) + dot_t(d_qkv[1], qkv_w[1]) + dot_t(d_qkv[2], qkv_w[2])
+    d_one, grad_gain_one, grad_bias_one = norm_back_one(d_normed_one)
+    d_inputs = d_after_self + d_one
+    late_sums.append(
+        lax.psum_scatter(
+            jnp.stack([grad_cout, grad_cq, grad_ck, grad_cv, grad_sout] + grads_qkv),
+            "dp",
+            scatter_dimension=1,
+            tiled=True,
+        )
+    )
+
+    d_blocks = slots_to_devices(d_third.T.reshape(PORTIONS, 32, GROUP, own_cells))
+    d_blocks = exchange_all(d_blocks.reshape(32, rows_own, own_cells), 6)
+    d_y3 = d_blocks.transpose(1, 0, 2).reshape(rows_own, number).astype(jnp.float32)
+    d_y3 = jnp.pad(d_y3, ((0, 0), (0, cells - number)))
+
+    def back_through(layer, d_y, n, r, x_all, w, cid):
+        dx, grad_w, sums = conv_block_back(layer, d_y, n, r, own_gb, masks, x_all, w.T, number)
+        total = reduce_all(dx.reshape(PORTIONS, 32, GROUP, cells), cid)
+        grad_w = grad_w.reshape(9, rows_own, features).transpose(1, 0, 2)
+        grad_w = grad_w.reshape(rows_own, examples, -1).transpose(1, 0, 2)
+        return d_y + total.reshape(rows_own, cells), grad_w, sums
+
+    d_y2, grad_conv_one, sums3 = back_through(2, d_y3, n3, r3, x2_all, convs[1], 7)
+    d_y1, grad_conv_zero, sums2 = back_through(1, d_y2, n2, r2, x1_all, convs[0], 8)
+    grad_patch, sums1 = first_block_back(d_y1, n1, r1, own_gb, pixels, number)
+    grad_patch = grad_patch.reshape(rows_own, examples, -1).transpose(1, 0, 2)
+    patch_rows = grad_patch.shape[2]
+    bn_grads = jnp.concatenate([sums1[:, :2], sums2[:, :2], sums3[:, :2]], 1).astype(LOW)
+    ln_grads = jnp.stack(
+        [
+            grad_gain_one,
+            grad_bias_one,
+            grad_gain_two,
+            grad_bias_two,
+            grad_gain_three,
+            grad_bias_three,
+        ]
+    ).astype(LOW)
+    ln_count = ln_grads.shape[0]
+    ln_blocks = ln_grads.reshape(ln_count, examples, -1).transpose(1, 0, 2)
+    ln_blocks = jnp.pad(ln_blocks, ((0, 0), (0, rows_own - ln_count), (0, 0)))
+    send_blocks = jnp.concatenate(
+        [
+            grad_conv_zero,
+            grad_conv_one,
+            grad_patch,
+            jnp.broadcast_to(bn_grads, (examples,) + bn_grads.shape),
+            ln_blocks,
+        ],
+        2,
+    )
+    got = swap_both(send_blocks, 9).transpose(1, 0, 2, 3).reshape(32, rows_own, -1)
+    conv_rows = w_conv.shape[1]
+    width = 2 * conv_rows + patch_rows
+    mixed = devices_to_slots(got[:, :, : width + 6].reshape(32, PORTIONS, GROUP, width + 6))
+    mixed = mixed.reshape(features, width + 6)
+    stem_grads = mixed[:, :width].T.astype(jnp.float32)
+    bn_part = lax.dynamic_slice_in_dim(mixed[:, width:], a_index * patch_rows, patch_rows, 0)
+    ln_part = jnp.sum(got[:, :ln_count, width + 6 :].astype(jnp.float32), 0)
+    norm_grads = jnp.concatenate([bn_part.T.astype(jnp.float32), ln_part], 0)
+
+    sums = jnp.concatenate(late_sums, 0)
+    sums = sums.astype(jnp.float32) + pair_swap(sums, 10).astype(jnp.float32)
+    down_sum = sums[:4].reshape(w_down.shape)
+    up_sum = jnp.concatenate([sums[4 + i] for i in range(4)], 1)
+    return (
+        result[None].astype(LOW),
+        d_inputs[None].astype(LOW),
+        prefix_back[None].astype(LOW),
+        stem_grads[2 * conv_rows :],
+        stem_grads[: 2 * conv_rows].reshape(w_conv.shape),
+        jnp.concatenate([sums[13], sums[14], sums[15]], 1),
+        sums[12],
+        sums[9],
+        jnp.concatenate([sums[10], sums[11]], 1),
+        sums[8],
+        up_sum,
+        down_sum,
+        norm_grads,
+    )
+
+
+def suits(mesh):
+    return mesh.shape["dp"] == 16 and mesh.shape["seq"] == 2
+
+
 def solution(mesh):
     return jax.shard_map(
-        on_device,
+        fast_device if suits(mesh) else general_device,
         mesh=mesh,
         in_specs=(
             P("dp", "seq", None),

time: 1810 us -> 829 us (0.46)
  waiting for transfers between devices: 1030 us -> 2.01 us
  Pallas kernels: 0 us -> 427 us
  blocking collectives: 288 us -> 0 us
  matrix products: 267 us -> 181 us
  local copies, waits for them, and re-layouts: 57.2 us -> 115 us
  other arithmetic: 97.1 us -> 62 us
  starting transfers between devices: 33.9 us -> 12.1 us
    reduce_scatter x7 -> x2, waiting for transfers between devices: 711 us -> 0.02 us  [the longest x1 0.02 us: fast_device(): lax.psum_scatter(jnp.stack([grad_cout, grad_cq, grad_ck, grad_cv, grad_so...]
    pallas_call x0 -> x17, Pallas kernels: none -> 427 us  [the longest x3 167 us: gather_all(): pl.pallas_call(gather_body, name='gather_all', out_shape=jax.ShapeDtypeSt...]
    psum x7 -> x0, blocking collectives: 250 us -> none  [the longest x3 123 us: batch_back(): lax.psum((jnp.sum(d_normed, 0), jnp.sum(d_normed * normed, 0)), ('dp', 's...]
    all_gather x9 -> x3, waiting for transfers between devices: 164 us -> 0.04 us  [the longest x1 0.02 us: fast_device(): lax.all_gather(jnp.stack([w_self_out, w_cross_q] + chunks(w_cross_kv) + [...]
    dot_general x80 -> x17, matrix products: 184 us -> 43.5 us  [dot_float(): return jnp.dot(left, right, preferred_element_type=jnp.float32)]
    psum x1 -> x0, waiting for transfers between devices: 79.9 us -> none  [on_device(): lax.psum(shard_sums[0].astype(jnp.bfloat16), 'seq').astype(jnp.float32)]
    unnamed x27 -> x5, waiting for transfers between devices: 61.1 us -> 0.08 us
    dot_general x0 -> x28, matrix products: none -> 51 us  [the longest x16 28.4 us: dot_t(): lax.dot_general(left, right, (((1,), (1,)), ((), ())), preferred_element_...]
  transfers between devices with their start and end apart: 34 -> 10, of which waited for: 15 -> 1; matrix products, arithmetic and copies ran while one was open for 21% -> 32% of each run, Pallas kernels for 0% -> 49%
where the time goes in v1:
time: 829 us; the launch traced here: 817 us
  Pallas kernels  427 us (52%)
  matrix products  181 us (22%)
  local copies, waits for them, and re-layouts  115 us (14%)
  other arithmetic  62 us (7%)
  between operations  17.5 us (2%)
  starting transfers between devices  12.1 us (1%)
    pallas_call x3, Pallas kernels, gather_all(): pl.pallas_call(gather_body, name='gather_all', out_shape=jax.ShapeDtypeSt...  167 us
    pallas_call x2, Pallas kernels, reduce_all(): pl.pallas_call(reduce_body, name='reduce_all', out_shape=jax.ShapeDtypeSt...  116 us
    unnamed x241, local copies, waits for them, and re-layouts  49.5 us
    dot_general x17, matrix products, dot_float(): return jnp.dot(left, right, preferred_element_type=jnp.float32)  43.5 us
    pallas_call x2, Pallas kernels, pair_swap(): pl.pallas_call(pair_body, name='pair_swap', out_shape=jax.ShapeDtypeStruc...  38.1 us
    pallas_call x1, Pallas kernels, swap_both(): pl.pallas_call(swap_both_body, name='swap_both', out_shape=jax.ShapeDtype...  29.2 us
    dot_general x16, matrix products, dot_t(): lax.dot_general(left, right, (((1,), (1,)), ((), ())), preferred_element_...  28.4 us
    pallas_call x2, Pallas kernels, exchange_all(): pl.pallas_call(exchange_body, name='exchange_all', out_shape=jax.ShapeDty...  27 us
  transfers between devices with their start and end apart: 10, of which 1 were waited for; matrix products, arithmetic and copies ran while one was open for 32% of the time, Pallas kernels for 49%

profile of v1, /device:TPU:0, one launch (start us, length us, event | category | flops | bytes accessed | tf_op | source)
XLA Modules:
  0.0 816.6 jit_solution(7141398026611802573)
XLA Ops:
  19.0 21.4 %swap_dp.1 = bf16[16,24,960]{2,1,0:T(8,128)(2,1)} custom-call(bf16[16,24,960]{2,1,0:T(8,128)(2,1)} %pad_maximum_fusion.8.x_ref), custom_call_target="tpu_custom_call" | custom-call | tf_op jit(solution)/shard_map/swap_dp/pallas_call | solution.py:271
  49.6 54.9 %gather_all.3 = bf16[3,32,98,256]{3,2,1,0:T(8,128)(2,1)} custom-call(bf16[3,98,256]{2,1,0:T(8,128)(2,1)} %bitcast.568), custom_call_target="tpu_custom_call" | custom-call | tf_op jit(solution)/shard_map/gather_all/pallas_call | solution.py:160
  110.6 9.4 %copy.343 = bf16[32,98,3,256]{3,2,1,0:T(4,128)(2,1)} copy(bf16[32,98,3,256]{3,1,0,2:T(8,128)(2,1)} %maximum_bitcast_fusion) | data formatting | bytes 9633792 | tf_op jit(solution)/shard_map/reshape | solution.py:1198
  120.0 5.5 copy.354
  129.0 58.6 %gather_all.4 = bf16[3,32,8,3200]{3,2,1,0:T(8,128)(2,1)} custom-call(bf16[3,8,3200]{2,1,0:T(8,128)(2,1)} %copy-done.6), custom_call_target="tpu_custom_call" | custom-call | tf_op jit(solution)/shard_map/gather_all/pallas_call | solution.py:160
  187.6 4.4 stem_conv.2
  192.7 53.3 %gather_all.5 = bf16[3,32,8,3200]{3,2,1,0:T(8,128)(2,1)} custom-call(bf16[3,8,3200]{2,1,0:T(8,128)(2,1)} %copy-done.7), custom_call_target="tpu_custom_call" | custom-call | tf_op jit(solution)/shard_map/gather_all/pallas_call | solution.py:160
  246.1 5.3 stem_conv.3
  252.7 9.3 %exchange_all.2 = bf16[32,24,196]{2,1,0:T(8,128)(2,1)} custom-call(bf16[32,24,196]{2,1,0:T(8,128)(2,1)} %bitcast.549), custom_call_target="tpu_custom_call" | custom-call | tf_op jit(solution)/shard_map/exchange_all/pallas_call | solution.py:378
  273.5 4.6 collective-permute-start.1
  293.7 14.4 %fusion.6 = (f32[12,512]{1,0:T(8,128)S(1)}, f32[12,512,1024]{2,1,0:T(8,128)}) fusion(pred[512,1024]{1,0:T(8,128)(4,1)} %and_and_fusion, bf16[512,12,64]{0,2,1:T(8,128)(2,1)} %bitcast.494, bf16[512,12,64]{0,2,1:T(8,128)(2,1)} %bitcast.499, bf16[512,12,64]{0,2,1:T(8,128)(2,1)} %collective-permute-done.1), kind=kOutput, calls=%fused_computation.11 | convolution fusion | flops 827320320 | bytes 28073984 | tf_op jit(solution)/shard_map/while/body/eval_jaxpr/qhd,khd->hqk/dot_general | solution.py:731
  308.1 11.8 %fusion = f32[12,512]{1,0:T(8,128)S(1)} fusion(f32[12,512]{1,0:T(8,128)S(1)} %get-tuple-element.276, f32[12,512,1024]{2,1,0:T(8,128)} %get-tuple-element.277, pred[512,1024]{1,0:T(8,128)(4,1)S(1)} %copy-done.26), kind=kLoop, calls=%fused_computation.6 | loop fusion | flops 25159680 | bytes 25739264 | tf_op jit(solution)/shard_map/while/body/eval_jaxpr/reduce_sum | solution.py:737
  320.9 12.8 %fusion.104 = bf16[12,64,512]{2,1,0:T(8,128)(2,1)} fusion(f32[12,512]{1,0:T(8,128)S(1)} %fusion, f32[12,512]{1,0:T(8,128)S(1)} %get-tuple-element.276, f32[12,512,1024]{2,1,0:T(8,128)} %get-tuple-element.277, pred[512,1024]{1,0:T(8,128)(4,1)S(1)} %copy-done.26, bf16[512,12,64]{0,2,1:T(8,128)(2,1)S(1)} %bitcast.524, ...), kind=kOutput, calls=%fused_computation.193 | convolution fusion | flops 840302592 | bytes 28098560 | tf_op jit(solution)/shard_map/while/body/eval_jaxpr/hqk,khd->qhd/dot_general | solution.py:739
  366.0 3.7 fusion.72
  369.7 4.2 fusion.62
  387.0 3.7 fusion.16
  390.7 6.4 multiply_reduce_fusion.1
  397.3 5.2 convolution_convert_fusion
  406.8 4.4 multiply_convert_fusion.1
  414.5 4.8 constant_dynamic-update-slice_fusion
  427.7 10.1 %pair_swap.2 = bf16[114,1536]{1,0:T(8,128)(2,1)} custom-call(bf16[114,1536]{1,0:T(8,128)(2,1)} %pad_maximum_fusion.13.x_ref), custom_call_target="tpu_custom_call" | custom-call | tf_op jit(solution)/shard_map/pair_swap/pallas_call | solution.py:409
  453.0 12.5 %fusion.26 = f32[1024,12,64]{0,2,1:T(8,128)S(1)} fusion(bf16[512,12,64]{0,2,1:T(8,128)(2,1)} %bitcast.525, f32[12,512]{1,0:T(8,128)S(1)} %log_add_fusion, f32[12,512,1024]{2,1,0:T(8,128)} %get-tuple-element.277, pred[512,1024]{1,0:T(8,128)(4,1)} %and_and_fusion), kind=kOutput, calls=%fused_computation.64 | convolution fusion | flops 830472192 | bytes 29646848 | tf_op jit(solution)/shard_map/while/body/eval_jaxpr/hqk,qhd->khd/dot_general | solution.py:761
  469.7 18.0 %multiply_reduce_fusion = (f32[12,512]{1,0:T(8,128)S(1)}, f32[12,512,1024]{2,1,0:T(8,128)}) fusion(f32[12,512]{1,0:T(8,128)S(1)} %log_add_fusion, f32[12,512,1024]{2,1,0:T(8,128)} %get-tuple-element.277, pred[512,1024]{1,0:T(8,128)(4,1)} %and_and_fusion, bf16[512,12,64]{0,2,1:T(8,128)(2,1)} %bitcast.526, bf16[512,12,64]{0,2,1:T(8,128)(2,1)} %bitcast.523, ...), kind=kOutput, calls=%fused_computation.1 | convolution fusion | flops 839903232 | bytes 53264384 | tf_op jit(solution)/shard_map/while/body/eval_jaxpr/qhd,khd->hqk/dot_general | solution.py:750
  487.7 17.8 %multiply_convert_fusion = bf16[12,512,1024]{2,1,0:T(8,128)(2,1)S(1)} fusion(f32[12,512,1024]{2,1,0:T(8,128)} %get-tuple-element.297, f32[12,512]{1,0:T(8,128)S(1)} %get-tuple-element.296, f32[12,512]{1,0:T(8,128)S(1)} %log_add_fusion, f32[12,512,1024]{2,1,0:T(8,128)} %get-tuple-element.277, pred[512,1024]{1,0:T(8,128)(4,1)} %and_and_fusion), kind=kLoop, calls=%fused_computation | loop fusion | flops 37748736 | bytes 63488000 | tf_op jit(solution)/shard_map/while/body/eval_jaxpr/convert_element_type | solution.py:752
  519.5 9.2 %multiply_convert_fusion.2 = bf16[12,64,512]{2,1,0:T(8,128)(2,1)S(1)} fusion(bf16[12,512,1024]{2,1,0:T(8,128)(2,1)} %copy-done.9, bf16[512,12,64]{0,2,1:T(8,128)(2,1)S(1)} %bitcast.500, bf16[512,12,64]{0,2,1:T(8,128)(2,1)} %collective-permute-done.1), kind=kOutput, calls=%fused_computation.128 | convolution fusion | flops 809238528 | bytes 14942208 | tf_op jit(solution)/shard_map/while/body/eval_jaxpr/hqk,khd->qhd/dot_general | solution.py:754
  549.9 17.6 %exchange_all.3 = bf16[32,24,98]{2,1,0:T(8,128)(2,1)} custom-call(bf16[32,24,98]{2,1,0:T(8,128)(2,1)} %copy_bitcast_fusion.4.x_ref), custom_call_target="tpu_custom_call" | custom-call | tf_op jit(solution)/shard_map/exchange_all/pallas_call | solution.py:378
  568.8 8.2 %stem_conv_back.2 = (bf16[768,3200]{1,0:T(8,128)(2,1)}, bf16[216,768]{1,0:T(8,128)(2,1)S(1)}, f32[24,128]{1,0:T(8,128)S(1)}) custom-call(f32[24,3200]{1,0:T(8,128)S(1)} %pad_convert_fusion.dy_ref, f32[24,3200]{1,0:T(8,128)S(1)} %get-tuple-element.139.n_ref, f32[24,128]{1,0:T(8,128)S(1)} %get-tuple-element.152.rstd_ref, f32[24,128]{1,0:T(8,128)S(1)} %copy-done.5, ...), custom_call_target="tpu_custom_call" | custom-call | tf_op jit(solution)/shard_map/stem_conv_back/pallas_call | solution.py:602
  579.4 64.5 %reduce_all.2 = f32[3,8,3200]{2,1,0:T(8,128)S(1)} custom-call(bf16[3,32,8,3200]{3,2,1,0:T(8,128)(2,1)S(1)} %bitcast.476), custom_call_target="tpu_custom_call" | custom-call | tf_op jit(solution)/shard_map/reduce_all/pallas_call | solution.py:228
  643.9 7.7 stem_conv_back.3
  654.0 51.6 %reduce_all.3 = f32[3,8,3200]{2,1,0:T(8,128)S(1)} custom-call(bf16[3,32,8,3200]{3,2,1,0:T(8,128)(2,1)S(1)} %bitcast.477), custom_call_target="tpu_custom_call" | custom-call | tf_op jit(solution)/shard_map/reduce_all/pallas_call | solution.py:228
  729.1 29.2 %swap_both.1 = bf16[2,16,24,966]{3,2,1,0:T(8,128)(2,1)} custom-call(bf16[16,24,966]{2,1,0:T(8,128)(2,1)} %concatenate.83.x_ref), custom_call_target="tpu_custom_call" | custom-call | tf_op jit(solution)/shard_map/swap_both/pallas_call | solution.py:334
  775.9 28.0 %pair_swap.3 = bf16[16,48,768]{2,1,0:T(8,128)(2,1)} custom-call(bf16[16,48,768]{2,1,0:T(8,128)(2,1)} %copy-done.28), custom_call_target="tpu_custom_call" | custom-call | tf_op jit(solution)/shard_map/pair_swap/pallas_call | solution.py:409
  (498 shorter events, 226.6 us)
Async XLA Ops:
  7.2 260.9 %all-gather.4.cloned.1.call-start = ((), (), s32[]{:S(2)}) async-start(), calls=%async_computation.2 | async-start | bytes 3760128 | tf_op jit(solution)/shard_map/all_gather | solution.py:1177
  8.3 7.7 copy-start.47
  8.3 7.7 copy-start.72
  9.1 324.6 %all-gather.6.cloned.1.call-start = ((), (), s32[]{:S(2)}) async-start(), calls=%async_computation.3 | async-start | bytes 11280384 | tf_op jit(solution)/shard_map/all_gather | solution.py:1178
  12.8 353.2 %all-gather.8.cloned.1.call-start = ((), (), s32[]{:S(2)}) async-start(), calls=%async_computation.4 | async-start | bytes 5013504 | tf_op jit(solution)/shard_map/all_gather | solution.py:1184
  12.8 252.2 %collective-permute-start.2 = (bf16[16,768]{1,0:T(8,128)(2,1)S(1)}, bf16[16,768]{1,0:T(8,128)(2,1)S(1)}, u32[]{:S(2)}, u32[]{:S(2)}) collective-permute-start(bf16[16,768]{1,0:T(8,128)(2,1)S(1)} %bitcast.587), channel_id=1, source_target_pairs={{0,1},{1,0},{2,3},{3,2},{4,5},{5,4},{6,7},{7,6},{8,9},{9,8},{10,11... | collective-permute-start | bytes 73736 | tf_op jit(solution)/shard_map/ppermute | solution.py:1217
  15.9 756.7 %reduce-scatter.3.cloned.1.call-start = ((), (), s32[]{:S(2)}) async-start(), calls=%async_computation.5 | async-start | bytes 10027008 | tf_op jit(solution)/shard_map/reduce_scatter | solution.py:1286
  19.0 26.3 %copy-start.14 = (bf16[1,512,768]{2,1,0:T(8,128)(2,1)S(1)}, bf16[1,512,768]{2,1,0:T(8,128)(2,1)}, u32[]{:S(2)}) copy-start(bf16[1,512,768]{2,1,0:T(8,128)(2,1)} %param.17) | copy-start | bytes 2359300
  45.5 239.7 %copy-start.77 = (f32[512]{0:T(512)}, f32[512]{0:T(512)S(1)}, u32[]{:S(2)}) copy-start(f32[512]{0:T(512)S(1)} %broadcast_multiply_fusion.2) | copy-start | bytes 6148
  45.9 239.3 %copy-start.85 = (f32[512]{0:T(512)}, f32[512]{0:T(512)S(1)}, u32[]{:S(2)}) copy-start(f32[512]{0:T(512)S(1)} %fusion.152) | copy-start | bytes 6148
  126.4 119.7 %copy-start.4 = (f32[24,128]{1,0:T(8,128)}, f32[24,128]{1,0:T(8,128)S(1)}, u32[]{:S(2)}) copy-start(f32[24,128]{1,0:T(8,128)S(1)} %pad.24.gb_ref) | copy-start | bytes 36868
  264.7 20.4 %copy-start.74 = (f32[768]{0:T(1024)}, f32[768]{0:T(1024)S(1)}, u32[]{:S(2)}) copy-start(f32[768]{0:T(1024)S(1)} %mul.468) | copy-start | bytes 9220
  264.8 20.3 %copy-start.88 = (f32[768]{0:T(1024)}, f32[768]{0:T(1024)S(1)}, u32[]{:S(2)}) copy-start(f32[768]{0:T(1024)S(1)} %add.354) | copy-start | bytes 9220
  273.5 20.2 %collective-permute-start.1 = (bf16[512,12,64]{0,2,1:T(8,128)(2,1)}, bf16[512,12,64]{0,2,1:T(8,128)(2,1)}, u32[]{:S(2)}, u32[]{:S(2)}) collective-permute-start(bf16[512,12,64]{0,2,1:T(8,128)(2,1)} %bitcast.498), channel_id=1, source_target_pairs={{0,1},{2,3},{4,5},{6,7},{8,9},{10,11},{12,13},{14,15},{16,17},{18,... | collective-permute-start | bytes 2359304 | tf_op jit(solution)/shard_map/ppermute | solution.py:648
  290.5 29.4 %collective-permute-start = (bf16[512,12,64]{0,2,1:T(8,128)(2,1)}, bf16[512,12,64]{0,2,1:T(8,128)(2,1)S(1)}, u32[]{:S(2)}, u32[]{:S(2)}) collective-permute-start(bf16[512,12,64]{0,2,1:T(8,128)(2,1)} %bitcast.522), channel_id=1, source_target_pairs={{0,1},{2,3},{4,5},{6,7},{8,9},{10,11},{12,13},{14,15},{16,17},{18,... | collective-permute-start | bytes 2359304 | tf_op jit(solution)/shard_map/ppermute | solution.py:648
  293.7 14.4 %copy-start.26 = (pred[512,1024]{1,0:T(8,128)(4,1)S(1)}, pred[512,1024]{1,0:T(8,128)(4,1)}, u32[]{:S(2)}) copy-start(pred[512,1024]{1,0:T(8,128)(4,1)} %and_and_fusion) | copy-start | bytes 1572868
  308.1 12.8 %copy-start.38 = (bf16[512,768]{0,1:T(8,128)(2,1)S(1)}, bf16[512,768]{0,1:T(8,128)(2,1)}, u32[]{:S(2)}) copy-start(bf16[512,768]{0,1:T(8,128)(2,1)} %copy.279) | copy-start | bytes 2359300
  338.3 8.2 %copy-start.33 = (bf16[228,768]{0,1:T(8,128)(2,1)}, bf16[228,768]{0,1:T(8,128)(2,1)S(1)}, u32[]{:S(2)}) copy-start(bf16[228,768]{0,1:T(8,128)(2,1)S(1)} %copy.306) | copy-start | bytes 1050628
  356.0 27.1 %copy-start.10 = (f32[512,768]{1,0:T(8,128)}, f32[512,768]{1,0:T(8,128)S(1)}, u32[]{:S(2)}) copy-start(f32[512,768]{1,0:T(8,128)S(1)} %get-tuple-element.283) | copy-start | bytes 4718596
  366.0 7.9 slice-start.5
  366.0 7.9 slice-start.6
  366.0 8.9 %slice-start.9 = ((s8[4718592]{0:T(1024)(128)(4,1)}), s8[4194304]{0:T(1024)(128)(4,1)S(1)}, s32[]{:S(2)}) async-start(s8[4718592]{0:T(1024)(128)(4,1)} %bitcast.577), calls=%async_computation.16 | async-start | bytes 8388608
  369.7 12.1 %copy-start.55 = (bf16[512,768]{1,0:T(8,128)(2,1)}, bf16[512,768]{1,0:T(8,128)(2,1)S(1)}, u32[]{:S(2)}) copy-start(bf16[512,768]{1,0:T(8,128)(2,1)S(1)} %fusion.72) | copy-start | bytes 2359300
  426.8 347.0 %reduce-scatter.5.cloned.1.call-start = ((), (), s32[]{:S(2)}) async-start(), calls=%async_computation.6 | async-start | bytes 10027008 | tf_op jit(solution)/shard_map/reduce_scatter | solution.py:1345
  468.4 70.0 %collective-permute-start.4 = (bf16[512,12,64]{0,2,1:T(8,128)(2,1)}, bf16[512,12,64]{0,2,1:T(8,128)(2,1)}, u32[]{:S(2)}, u32[]{:S(2)}) collective-permute-start(bf16[512,12,64]{0,2,1:T(8,128)(2,1)} %slice.544), channel_id=1, source_target_pairs={{1,0},{3,2},{5,4},{7,6},{9,8},{11,10},{13,12},{15,14},{17,16},{19,... | collective-permute-start | bytes 2359304 | tf_op jit(solution)/shard_map/ppermute | solution.py:648
  487.7 17.9 %copy-start.27 = (bf16[512,768]{0,1:T(8,128)(2,1)S(1)}, bf16[512,768]{0,1:T(8,128)(2,1)}, u32[]{:S(2)}) copy-start(bf16[512,768]{0,1:T(8,128)(2,1)} %copy.280) | copy-start | bytes 2359300
  511.1 23.7 %collective-permute-start.3 = (bf16[512,12,64]{0,2,1:T(8,128)(2,1)}, bf16[512,12,64]{0,2,1:T(8,128)(2,1)}, u32[]{:S(2)}, u32[]{:S(2)}) collective-permute-start(bf16[512,12,64]{0,2,1:T(8,128)(2,1)} %slice.545), channel_id=1, source_target_pairs={{1,0},{3,2},{5,4},{7,6},{9,8},{11,10},{13,12},{15,14},{17,16},{19,... | collective-permute-start | bytes 2359304 | tf_op jit(solution)/shard_map/ppermute | solution.py:648
  517.9 10.8 %copy-start.39 = (bf16[114,1536]{1,0:T(8,128)(2,1)}, bf16[114,1536]{1,0:T(8,128)(2,1)S(1)}, u32[]{:S(2)}) copy-start(bf16[114,1536]{1,0:T(8,128)(2,1)S(1)} %fusion.139) | copy-start | bytes 1050628
  519.5 10.8 %copy-start.52 = (bf16[12,64,512]{2,1,0:T(8,128)(2,1)S(1)}, bf16[12,64,512]{2,1,0:T(8,128)(2,1)}, u32[]{:S(2)}) copy-start(bf16[12,64,512]{2,1,0:T(8,128)(2,1)} %fusion.104) | copy-start | bytes 2359300
  548.7 20.1 %copy-start.5 = (f32[24,128]{1,0:T(8,128)S(1)}, f32[24,128]{1,0:T(8,128)}, u32[]{:S(2)}) copy-start(f32[24,128]{1,0:T(8,128)} %copy-done.4) | copy-start | bytes 36868
  579.4 126.3 %slice-start = ((s8[4915200]{0:T(1024)(128)(4,1)}), s8[4194304]{0:T(1024)(128)(4,1)S(1)}, s32[]{:S(2)}) async-start(s8[4915200]{0:T(1024)(128)(4,1)} %bitcast.474), calls=%async_computation.7 | async-start | bytes 8388608
  643.9 61.8 %slice-start.1 = ((s8[4915200]{0:T(1024)(128)(4,1)}), s8[720896]{0:T(1024)(128)(4,1)S(1)}, s32[]{:S(2)}) async-start(s8[4915200]{0:T(1024)(128)(4,1)} %bitcast.474), calls=%async_computation.8 | async-start | bytes 1441792
  (92 other events, 223.0 us)
Sparse Core Ops, SparseCore 0:
  10.9 66.1 all-gather.3
  80.0 101.2 all-gather.5
  183.6 68.2 all-gather.7
  426.9 117.1 reduce-scatter.2
  548.6 146.0 reduce-scatter.4

commit v2 on v1

--- a/solution.py
+++ b/solution.py
@@ -283,12 +283,16 @@
     )(x)
 
 
-def swap_both_body(x_ref, o_ref, send_sem, recv_sem, pass_sem, got_sem, own_sem):
+def swap_both_body(
+    x_ref, half_ref, o_ref, both_ref, send_sem, recv_sem, pass_sem, got_sem, own_sem, half_sem
+):
     a, s = lax.axis_index("dp"), lax.axis_index("seq")
     count = x_ref.shape[0]
     greet([(lax.rem(a + j, count), s) for j in range(1, count)] + [(a, 1 - s)])
     own = pltpu.make_async_copy(x_ref.at[a], o_ref.at[s, a], own_sem)
     own.start()
+    own_half = pltpu.make_async_copy(half_ref, both_ref.at[s], half_sem.at[0])
+    own_half.start()
     copies = []
 
     def pass_on(src, slot, j):
@@ -316,6 +320,16 @@
         )
         copy.start()
         copies.append(copy)
+    half = pltpu.make_async_remote_copy(
+        src_ref=half_ref,
+        dst_ref=both_ref.at[s],
+        send_sem=half_sem.at[1],
+        recv_sem=half_sem.at[2],
+        device_id=(a, 1 - s),
+        device_id_type=MESH,
+    )
+    half.start()
+    copies.append(half)
     for j in range(1, count):
         source = lax.rem(a - j + count, count)
         got = o_ref.at[s, source]
@@ -324,22 +338,28 @@
     for j in range(count):
         got = o_ref.at[1 - s, lax.rem(a - j + count, count)]
         arrived(got, got_sem.at[j])
+    arrived(both_ref.at[1 - s], half_sem.at[2])
     for copy in copies:
         copy.wait_send()
     own.wait()
-
-
-def swap_both(x, cid):
+    own_half.wait()
+
+
+def swap_both(x, half, cid):
     count = x.shape[0]
     return pl.pallas_call(
         swap_both_body,
         name="swap_both",
-        out_shape=jax.ShapeDtypeStruct((2,) + x.shape, x.dtype),
-        in_specs=[pl.BlockSpec(memory_space=pltpu.HBM)],
-        out_specs=pl.BlockSpec(memory_space=pltpu.HBM),
-        scratch_shapes=[pltpu.SemaphoreType.DMA((count,))] * 4 + [pltpu.SemaphoreType.DMA],
+        out_shape=(
+            jax.ShapeDtypeStruct((2,) + x.shape, x.dtype),
+            jax.ShapeDtypeStruct((2,) + half.shape, half.dtype),
+        ),
+        in_specs=[pl.BlockSpec(memory_space=pltpu.HBM)] * 2,
+        out_specs=(pl.BlockSpec(memory_space=pltpu.HBM),) * 2,
+        scratch_shapes=[pltpu.SemaphoreType.DMA((count,))] * 4
+        + [pltpu.SemaphoreType.DMA, pltpu.SemaphoreType.DMA((3,))],
         compiler_params=pltpu.CompilerParams(collective_id=cid, has_side_effects=True),
-    )(x)
+    )(x, half)
 
 
 def exchange_body(x_ref, o_ref, send_sem, recv_sem, own_sem):
@@ -463,15 +483,7 @@
         x_ref[p] = y[GROUP * p : GROUP * (p + 1)].astype(x_ref.dtype)
 
 
-def first_body(number, p_ref, w_ref, gb_ref, m_ref, n_ref, rstd_ref, y_ref, x_ref, v_ref):
-    cells = p_ref.shape[0]
-    for start in range(0, cells, CHUNK):
-        v_ref[:, start : start + CHUNK] = lax.dot_general(
-            w_ref[...],
-            p_ref[start : start + CHUNK, :],
-            (((1,), (1,)), ((), ())),
-            preferred_element_type=jnp.float32,
-        )
+def first_body(number, v_ref, gb_ref, m_ref, n_ref, rstd_ref, y_ref, x_ref):
     normed, rstd, act = norm_act(v_ref[...], m_ref[9:10, :], gb_ref[:, 0:1], gb_ref[:, 1:2], number)
     n_ref[...] = normed
     rstd_ref[...] = jnp.broadcast_to(rstd, rstd_ref.shape)
@@ -557,15 +569,15 @@
     lanes = lax.broadcasted_iota(jnp.int32, s_ref.shape, 1)
     s_ref[...] = jnp.where(lanes == 0, d_gain, d_bias)
     g_ref[...] = jnp.dot(
-        dv.astype(p_ref.dtype), p_ref[...], preferred_element_type=jnp.float32
+        dv[:, : p_ref.shape[0]].astype(p_ref.dtype), p_ref[...], preferred_element_type=jnp.float32
     ).astype(g_ref.dtype)
 
 
 BIG = pltpu.CompilerParams(vmem_limit_bytes=48 << 20)
 
 
-def first_block(pixels, w, gb, masks, number):
-    rows, cells = w.shape[0], pixels.shape[0]
+def first_block(values, gb, masks, number):
+    rows, cells = values.shape
     return pl.pallas_call(
         functools.partial(first_body, number),
         name="stem_first",
@@ -575,9 +587,8 @@
             jax.ShapeDtypeStruct((rows, cells), jnp.float32),
             jax.ShapeDtypeStruct((PORTIONS, GROUP, cells), LOW),
         ),
-        scratch_shapes=[pltpu.VMEM((rows, cells), jnp.float32)],
         compiler_params=BIG,
-    )(pixels, w, gb, masks)
+    )(values, gb, masks)
 
 
 def conv_block(layer, x_all, w, gb, masks, y, number):
@@ -1102,6 +1113,151 @@
     )
 
 
+PAIR = 128
+
+
+def head_lanes(array, which, width):
+    lanes = lax.broadcasted_iota(jnp.int32, array.shape, 1)
+    return jnp.where((lanes >= which * width) & (lanes < (which + 1) * width), array, 0)
+
+
+def scores_t(keys, q_head):
+    return lax.dot_general(
+        keys, q_head, (((1,), (1,)), ((), ())), preferred_element_type=jnp.float32
+    )
+
+
+def masked_scores(kind, info_ref, ok_ref, keys, q_head):
+    if kind == "cross":
+        scores = scores_t(keys, q_head)
+        return jnp.where(ok_ref[:, 0:1] > 0, scores, -1e9)
+    half = keys.shape[0] // 2
+    before = scores_t(keys[:half], q_head)
+    own = scores_t(keys[half:], q_head)
+    before = jnp.where(info_ref[0] > 0, before, -1e9)
+    key_at = lax.broadcasted_iota(jnp.int32, own.shape, 0)
+    query_at = lax.broadcasted_iota(jnp.int32, own.shape, 1)
+    own = jnp.where((key_at <= query_at) & (key_at < info_ref[1]), own, -1e9)
+    return jnp.concatenate([before, own], 0)
+
+
+def attend_body(kind, width, info_ref, ok_ref, q_ref, k_ref, v_ref, o_ref, lse_ref):
+    keys, values = k_ref[...], v_ref[...]
+    outs = []
+    for which in range(PAIR // width):
+        q_head = head_lanes(q_ref[...], which, width)
+        scores = masked_scores(kind, info_ref, ok_ref, keys, q_head)
+        top = jnp.max(scores, 0, keepdims=True)
+        weights = jnp.exp(scores - top)
+        total = jnp.sum(weights, 0, keepdims=True)
+        lse_ref[0, which : which + 1, :] = top + jnp.log(total)
+        out_t = lax.dot_general(
+            head_lanes(values, which, width),
+            weights.astype(LOW),
+            (((0,), (0,)), ((), ())),
+            preferred_element_type=jnp.float32,
+        )
+        outs.append(out_t / total)
+    o_ref[...] = (outs[0] + outs[1]).T.astype(o_ref.dtype)
+
+
+def attend_back_body(
+    kind, width, scale, info_ref, ok_ref, q_ref, k_ref, v_ref, do_ref, lse_ref, dq_ref, dk_ref, dv_ref
+):
+    keys, values = k_ref[...], v_ref[...]
+    dq_t, dk, dv = None, None, None
+    for which in range(PAIR // width):
+        q_head = head_lanes(q_ref[...], which, width)
+        do_head = head_lanes(do_ref[...], which, width)
+        scores = masked_scores(kind, info_ref, ok_ref, keys, q_head)
+        probs = jnp.exp(scores - lse_ref[0, which : which + 1, :])
+        d_probs = scores_t(values, do_head)
+        delta = jnp.sum(probs * d_probs, 0, keepdims=True)
+        ds = (probs * (d_probs - delta)).astype(LOW)
+        part_k = jnp.dot(ds, q_head, preferred_element_type=jnp.float32)
+        part_v = jnp.dot(probs.astype(LOW), do_head, preferred_element_type=jnp.float32)
+        part_q = lax.dot_general(
+            head_lanes(keys, which, width),
+            ds,
+            (((0,), (0,)), ((), ())),
+            preferred_element_type=jnp.float32,
+        )
+        dk = part_k if dk is None else dk + part_k
+        dv = part_v if dv is None else dv + part_v
+        dq_t = part_q if dq_t is None else dq_t + part_q
+    dq_ref[...] = (dq_t * scale).T.astype(dq_ref.dtype)
+    dk_ref[...] = dk.astype(dk_ref.dtype)
+    dv_ref[...] = dv.astype(dv_ref.dtype)
+
+
+def attention_specs(rows, keys, ok):
+    return [
+        pl.BlockSpec(memory_space=pltpu.SMEM),
+        pl.BlockSpec(ok.shape, lambda i: (0, 0)),
+        pl.BlockSpec((rows, PAIR), lambda i: (0, i)),
+        pl.BlockSpec((keys, PAIR), lambda i: (0, i)),
+        pl.BlockSpec((keys, PAIR), lambda i: (0, i)),
+    ]
+
+
+def attend(kind, info, ok, q, k, v):
+    rows, features = q.shape
+    keys = k.shape[0]
+    width = features // HEADS
+    pairs = features // PAIR
+    return pl.pallas_call(
+        functools.partial(attend_body, kind, width),
+        name=kind + "_attend",
+        grid=(pairs,),
+        in_specs=attention_specs(rows, keys, ok),
+        out_specs=(
+            pl.BlockSpec((rows, PAIR), lambda i: (0, i)),
+            pl.BlockSpec((1, 8, rows), lambda i: (i, 0, 0)),
+        ),
+        out_shape=(
+            jax.ShapeDtypeStruct((rows, features), LOW),
+            jax.ShapeDtypeStruct((pairs, 8, rows), jnp.float32),
+        ),
+        compiler_params=BIG,
+        cost_estimate=pl.CostEstimate(
+            flops=4 * rows * keys * features, bytes_accessed=2 * (2 * rows + 2 * keys) * features,
+            transcendentals=rows * keys * HEADS,
+        ),
+    )(info, ok, q, k, v)
+
+
+def attend_grads(kind, info, ok, q, k, v, d_out, lse, scale):
+    rows, features = q.shape
+    keys = k.shape[0]
+    width = features // HEADS
+    pairs = features // PAIR
+    return pl.pallas_call(
+        functools.partial(attend_back_body, kind, width, scale),
+        name=kind + "_attend_back",
+        grid=(pairs,),
+        in_specs=attention_specs(rows, keys, ok)
+        + [
+            pl.BlockSpec((rows, PAIR), lambda i: (0, i)),
+            pl.BlockSpec((1, 8, rows), lambda i: (i, 0, 0)),
+        ],
+        out_specs=(
+            pl.BlockSpec((rows, PAIR), lambda i: (0, i)),
+            pl.BlockSpec((keys, PAIR), lambda i: (0, i)),
+            pl.BlockSpec((keys, PAIR), lambda i: (0, i)),
+        ),
+        out_shape=(
+            jax.ShapeDtypeStruct((rows, features), LOW),
+            jax.ShapeDtypeStruct((keys, features), jnp.float32),
+            jax.ShapeDtypeStruct((keys, features), jnp.float32),
+        ),
+        compiler_params=BIG,
+        cost_estimate=pl.CostEstimate(
+            flops=10 * rows * keys * features, bytes_accessed=2 * (3 * rows + 6 * keys) * features,
+            transcendentals=rows * keys * HEADS,
+        ),
+    )(info, ok, q, k, v, d_out, lse)
+
+
 def low_dot(left, right):
     return dot_float(left, right).astype(LOW)
 
@@ -1114,10 +1270,9 @@
     return lax.dot_general(left, right, (((0,), (0,)), ((), ())), preferred_element_type=jnp.float32)
 
 
-def stem_weights(w_patch, w_conv, norm_params, s):
-    depth, conv_rows, patch_rows = w_conv.shape[0], w_conv.shape[1], w_patch.shape[0]
-    features = w_patch.shape[1]
-    flat = jnp.concatenate([w_conv.reshape(-1, features), w_patch], 0).T
+def stem_weights(w_conv, norm_params, s):
+    depth, conv_rows, features = w_conv.shape
+    flat = w_conv.reshape(-1, features).T
     blocks = slots_to_devices(flat.reshape(PORTIONS, 32, GROUP, flat.shape[1]))
     blocks = blocks.reshape(16, 2, PORTIONS * GROUP, flat.shape[1])
     blocks = lax.dynamic_index_in_dim(blocks, s, 1, keepdims=False)
@@ -1130,11 +1285,8 @@
         part = got[:, :, layer * conv_rows : (layer + 1) * conv_rows]
         part = part.transpose(1, 0, 2).reshape(rows, 9, features).transpose(1, 0, 2)
         convs.append(part.reshape(9 * rows, features))
-    at = depth * conv_rows
-    patch = got[:, :, at : at + patch_rows].transpose(1, 0, 2).reshape(rows, -1)
-    at = at + patch_rows
-    norms = got[:, : norm_params.shape[0], at:].transpose(1, 0, 2).reshape(norm_params.shape[0], -1)
-    return convs, patch, norms
+    norms = got[:, : norm_params.shape[0], depth * conv_rows :]
+    return convs, norms.transpose(1, 0, 2).reshape(norm_params.shape[0], -1)
 
 
 def own_columns(norms):
@@ -1174,7 +1326,10 @@
     def chunks(w):
         return [w[:, i * features : (i + 1) * features] for i in range(w.shape[1] // features)]
 
-    qkv_w = lax.all_gather(jnp.stack(chunks(w_self_qkv)), "dp", axis=1, tiled=True)
+    first_w = lax.all_gather(
+        jnp.stack([w_patch] + chunks(w_self_qkv)), "dp", axis=1, tiled=True
+    )
+    patch_w, qkv_w = first_w[0], first_w[1:]
     rest_w = lax.all_gather(
         jnp.stack([w_self_out, w_cross_q] + chunks(w_cross_kv) + [w_cross_out] + chunks(w_up)),
         "dp",
@@ -1186,24 +1341,30 @@
     up_ws = [rest_w[5 + i] for i in range(4)]
     down_ws = [down_w[i * features : (i + 1) * features] for i in range(4)]
 
-    convs, patch_w, norms_low = stem_weights(w_patch, w_conv, norm_params, s_index)
+    convs, norms_low = stem_weights(w_conv, norm_params, s_index)
     norms = norms_low.astype(jnp.float32)
     own_gb = own_columns(norms[:6])
     own_cells = patches.shape[1]
     number = own_cells * examples * halves
     cells = -(-number // CHUNK) * CHUNK
+    rows_own = PORTIONS * GROUP
+    grid = halves * own_cells
     masks = jnp.asarray(tap_masks(cells, examples))
-    pixels_split = patches[0].reshape(own_cells, PORTIONS, -1).transpose(1, 0, 2)
-    pixels = slots_to_devices(gather_all(pixels_split, 1))
-    pixels = pixels.transpose(0, 2, 1, 3).reshape(number, -1)
-    pixels = jnp.pad(pixels, ((0, cells - number), (0, 0)))
-    n1, r1, y1, x1 = first_block(pixels, patch_w, own_gb, masks, number)
+    late_patches = lax.optimization_barrier((patches[0], down_w))[0]
+    pixels = lax.all_gather(late_patches, ("dp", "seq"), axis=0, tiled=True)
+
+    def to_channels(rows_by_channel, cid):
+        blocks = slots_to_devices(rows_by_channel.T.reshape(PORTIONS, 32, GROUP, own_cells))
+        blocks = exchange_all(blocks.reshape(32, rows_own, own_cells), cid)
+        blocks = blocks.transpose(1, 0, 2).reshape(rows_own, number)
+        return jnp.pad(blocks, ((0, 0), (0, cells - number)))
+
+    v1 = to_channels(dot_float(patches[0], patch_w), 1)
+    n1, r1, y1, x1 = first_block(v1, own_gb, masks, number)
     x1_all = gather_all(x1, 2).reshape(features, cells)
     n2, r2, y2, x2 = conv_block(1, x1_all, convs[0], own_gb, masks, y1, number)
     x2_all = gather_all(x2, 3).reshape(features, cells)
     n3, r3, y3, x3 = conv_block(2, x2_all, convs[1], own_gb, masks, y2, number)
-    rows_own = PORTIONS * GROUP
-    grid = halves * own_cells
     out_blocks = x3.reshape(rows_own, cells)[:, :number].reshape(rows_own, examples, grid)
     out_blocks = jnp.broadcast_to(
         out_blocks.transpose(1, 0, 2)[:, None], (examples, halves, rows_own, grid)
@@ -1226,40 +1387,28 @@
     memory = jnp.concatenate([prefix_all, patch_all], 0)
     mem_rows = memory.shape[0]
     prefix_total = prefix_all.shape[0]
-    mem_keys = heads_of(low_dot(memory, ck_w))
-    mem_values = heads_of(low_dot(memory, cv_w))
-    slot_ids = jnp.arange(mem_rows, dtype=jnp.int32)
-    mem_allowed = (slot_ids >= prefix_total) | (slot_ids < prefix_count[0])
-
-    def cross_allow(first_row, block_rows):
-        return jnp.broadcast_to(mem_allowed[None], (block_rows, mem_rows))
+    mem_padded = jnp.pad(memory, ((0, -mem_rows % 128), (0, 0)))
+    mem_keys = low_dot(mem_padded, ck_w)
+    mem_values = low_dot(mem_padded, cv_w)
+    slot_ids = jnp.arange(mem_padded.shape[0], dtype=jnp.int32)
+    mem_ok = (slot_ids < mem_rows) & ((slot_ids >= prefix_total) | (slot_ids < prefix_count[0]))
+    mem_ok = jnp.broadcast_to(mem_ok.astype(jnp.float32)[:, None], (mem_padded.shape[0], 128))
 
     inputs = captions[0].astype(jnp.float32)
     row_count = inputs.shape[0]
     low_one = layer_norm(inputs, norms[6], norms[7]).astype(LOW)
-    queries, own_keys, own_values = (heads_of(low_dot(low_one, qkv_w[i])) for i in range(3))
+    queries = (dot_float(low_one, qkv_w[0]).astype(LOW) * score_scale).astype(LOW)
+    own_keys, own_values = low_dot(low_one, qkv_w[1]), low_dot(low_one, qkv_w[2])
     got_keys, got_values = passed_along((own_keys, own_values), "seq", 1)
     all_keys = jnp.concatenate([got_keys, own_keys], 0)
     all_values = jnp.concatenate([got_values, own_values], 0)
-    ids = jnp.arange(row_count, dtype=jnp.int32)
-    key_pos = jnp.concatenate([(s_index - 1) * row_count + ids, s_index * row_count + ids], 0)
-    length_one = caption_len[0]
-
-    def self_allow(first_row, block_rows):
-        query_pos = s_index * row_count + first_row + jnp.arange(block_rows, dtype=jnp.int32)
-        return (
-            (key_pos[None] <= query_pos[:, None])
-            & (key_pos[None] >= 0)
-            & (key_pos[None] < length_one)
-        )
-
-    self_out, self_total = run_attention(queries, all_keys, all_values, self_allow, score_scale)
-    self_low = self_out.reshape(row_count, features).astype(LOW)
+    info = jnp.stack([s_index, caption_len[0] - s_index * row_count]).astype(jnp.int32)
+    no_ok = jnp.zeros((8, 128), jnp.float32)
+    self_low, self_lse = attend("self", info, no_ok, queries, all_keys, all_values)
     after_self = inputs + dot_float(self_low, sout_w)
     low_two = layer_norm(after_self, norms[8], norms[9]).astype(LOW)
-    cross_q = heads_of(low_dot(low_two, cq_w))
-    cross_out, cross_total = run_attention(cross_q, mem_keys, mem_values, cross_allow, score_scale)
-    cross_low = cross_out.reshape(row_count, features).astype(LOW)
+    cross_q = (dot_float(low_two, cq_w).astype(LOW) * score_scale).astype(LOW)
+    cross_low, cross_lse = attend("cross", info, mem_ok, cross_q, mem_keys, mem_values)
     after_cross = after_self + dot_float(cross_low, cout_w)
     low_three = layer_norm(after_cross, norms[10], norms[11]).astype(LOW)
     ups = [dot_float(low_three, w) for w in up_ws]
@@ -1285,7 +1434,7 @@
     late_sums = [
         lax.psum_scatter(
             jnp.concatenate([down_parts, jnp.stack(grads_up)], 0),
-            "dp",
+            ("dp", "seq"),
             scatter_dimension=1,
             tiled=True,
         )
@@ -1293,18 +1442,15 @@
     d_after_cross = out_grad + d_three
     cross_grad_low = d_after_cross.astype(LOW)
     grad_cout = t_dot(cross_low, cross_grad_low).astype(LOW)
-    d_cross = heads_of(dot_t(cross_grad_low, cout_w).astype(LOW))
-    d_cross_q, d_mem_keys, d_mem_values = run_back(
-        cross_q, mem_keys, mem_values, cross_allow, score_scale, d_cross, cross_total
-    )
-    d_cross_low = d_cross_q.reshape(row_count, features).astype(LOW)
+    d_cross = dot_t(cross_grad_low, cout_w).astype(LOW)
+    d_cross_low, d_mem_keys, d_mem_values = attend_grads(
+        "cross", info, mem_ok, cross_q, mem_keys, mem_values, d_cross, cross_lse, score_scale
+    )
     grad_cq = t_dot(low_two, d_cross_low).astype(LOW)
     unused_two, norm_back_two = jax.vjp(layer_norm, after_self, norms[8], norms[9])
     d_two, grad_gain_two, grad_bias_two = norm_back_two(dot_t(d_cross_low, cq_w))
     d_after_self = d_after_cross + d_two
-    d_memory = jnp.concatenate(
-        [d_mem_keys.reshape(mem_rows, features), d_mem_values.reshape(mem_rows, features)], 1
-    )
+    d_memory = jnp.concatenate([d_mem_keys, d_mem_values], 1)
 
     def half_of(array, which):
         return jnp.concatenate(
@@ -1326,16 +1472,16 @@
 
     self_grad_low = d_after_self.astype(LOW)
     grad_sout = t_dot(self_low, self_grad_low).astype(LOW)
-    d_self = heads_of(dot_t(self_grad_low, sout_w).astype(LOW))
-    d_query, d_all_keys, d_all_values = run_back(
-        queries, all_keys, all_values, self_allow, score_scale, d_self, self_total
+    d_self = dot_t(self_grad_low, sout_w).astype(LOW)
+    d_query, d_all_keys, d_all_values = attend_grads(
+        "self", info, no_ok, queries, all_keys, all_values, d_self, self_lse, score_scale
     )
     back_keys, back_values = passed_along(
         (d_all_keys[:row_count].astype(LOW), d_all_values[:row_count].astype(LOW)), "seq", -1
     )
     own_dkeys = d_all_keys[row_count:] + back_keys.astype(jnp.float32)
     own_dvalues = d_all_values[row_count:] + back_values.astype(jnp.float32)
-    d_qkv = [g.reshape(row_count, features).astype(LOW) for g in (d_query, own_dkeys, own_dvalues)]
+    d_qkv = [g.astype(LOW) for g in (d_query, own_dkeys, own_dvalues)]
     grads_qkv = [t_dot(low_one, g).astype(LOW) for g in d_qkv]
     unused_one, norm_back_one = jax.vjp(layer_norm, inputs, norms[6], norms[7])
     d_normed_one = dot_t(d_qkv[0], qkv_w[0]) + dot_t(d_qkv[1], qkv_w[1]) + dot_t(d_qkv[2], qkv_w[2])
@@ -1344,16 +1490,13 @@
     late_sums.append(
         lax.psum_scatter(
             jnp.stack([grad_cout, grad_cq, grad_ck, grad_cv, grad_sout] + grads_qkv),
-            "dp",
+            ("dp", "seq"),
             scatter_dimension=1,
             tiled=True,
         )
     )
 
-    d_blocks = slots_to_devices(d_third.T.reshape(PORTIONS, 32, GROUP, own_cells))
-    d_blocks = exchange_all(d_blocks.reshape(32, rows_own, own_cells), 6)
-    d_y3 = d_blocks.transpose(1, 0, 2).reshape(rows_own, number).astype(jnp.float32)
-    d_y3 = jnp.pad(d_y3, ((0, 0), (0, cells - number)))
+    d_y3 = to_channels(d_third, 6).astype(jnp.float32)
 
     def back_through(layer, d_y, n, r, x_all, w, cid):
         dx, grad_w, sums = conv_block_back(layer, d_y, n, r, own_gb, masks, x_all, w.T, number)
@@ -1391,7 +1534,10 @@
         ],
         2,
     )
-    got = swap_both(send_blocks, 9).transpose(1, 0, 2, 3).reshape(32, rows_own, -1)
+    sums = jnp.concatenate(late_sums, 0)
+    got, sums_both = swap_both(send_blocks, sums, 9)
+    got = got.transpose(1, 0, 2, 3).reshape(32, rows_own, -1)
+    sums = sums_both.transpose(1, 0, 2, 3).reshape(sums.shape[0], -1, features).astype(jnp.float32)
     conv_rows = w_conv.shape[1]
     width = 2 * conv_rows + patch_rows
     mixed = devices_to_slots(got[:, :, : width + 6].reshape(32, PORTIONS, GROUP, width + 6))
@@ -1401,8 +1547,6 @@
     ln_part = jnp.sum(got[:, :ln_count, width + 6 :].astype(jnp.float32), 0)
     norm_grads = jnp.concatenate([bn_part.T.astype(jnp.float32), ln_part], 0)
 
-    sums = jnp.concatenate(late_sums, 0)
-    sums = sums.astype(jnp.float32) + pair_swap(sums, 10).astype(jnp.float32)
     down_sum = sums[:4].reshape(w_down.shape)
     up_sum = jnp.concatenate([sums[4 + i] for i in range(4)], 1)
     return (

time: 829 us -> 747 us (0.901)
  matrix products: 181 us -> 101 us
  other arithmetic: 62 us -> 25 us
  Pallas kernels: 427 us -> 455 us
  waiting for transfers between devices: 2.01 us -> 29.7 us
  local copies, waits for them, and re-layouts: 115 us -> 94.9 us
    dot_general x12 -> x0, matrix products: 86.4 us -> none  [the longest x2 24.3 us: attend_back(): jnp.einsum('qhd,khd->hqk', grad_out, value_rows, preferred_element_type=j...]
    pallas_call x1 -> x5, Pallas kernels: 29.2 us -> 84.1 us  [the longest x1 33.8 us: swap_both(): pl.pallas_call(swap_both_body, name='swap_both', out_shape=(jax.ShapeDtyp...]
    pallas_call x3 -> x2, Pallas kernels: 167 us -> 119 us  [gather_all(): pl.pallas_call(gather_body, name='gather_all', out_shape=jax.ShapeDtypeSt...]
    pallas_call x2 -> x3, Pallas kernels: 27 us -> 58.4 us  [exchange_all(): pl.pallas_call(exchange_body, name='exchange_all', out_shape=jax.ShapeDty...]
    all_gather x1 -> x2, waiting for transfers between devices: 0.02 us -> 28.9 us  [the longest x1 28.8 us: fast_device(): lax.all_gather(jnp.stack([w_patch] + chunks(w_self_qkv)), 'dp', axis=1, t...]
    pallas_call x2, Pallas kernels: 116 us -> 89.6 us  [reduce_all(): pl.pallas_call(reduce_body, name='reduce_all', out_shape=jax.ShapeDtypeSt...]
    convert_element_type x4 -> x3, other arithmetic: 25.1 us -> 0.76 us  [the longest x1 0.57 us: fast_device(): mem_ok.astype(jnp.float32)[:, None]]
    pallas_call x2 -> x1, Pallas kernels: 38.1 us -> 54.6 us  [pair_swap(): pl.pallas_call(pair_body, name='pair_swap', out_shape=jax.ShapeDtypeStruc...]
  transfers between devices with their start and end apart: 10 -> 11, of which waited for: 1 -> 1; matrix products, arithmetic and copies ran while one was open for 32% -> 24% of each run, Pallas kernels for 49% -> 57%
where the time goes in v2:
time: 747 us; the launch traced here: 738 us
  Pallas kernels  455 us (61%)
  matrix products  101 us (14%)
  local copies, waits for them, and re-layouts  94.9 us (13%)
  waiting for transfers between devices  29.7 us (4%)
  other arithmetic  25 us (3%)
  between operations  18.6 us (2%)
  starting transfers between devices  13.5 us (2%)
    pallas_call x2, Pallas kernels, gather_all(): pl.pallas_call(gather_body, name='gather_all', out_shape=jax.ShapeDtypeSt...  119 us
    pallas_call x2, Pallas kernels, reduce_all(): pl.pallas_call(reduce_body, name='reduce_all', out_shape=jax.ShapeDtypeSt...  89.6 us
    pallas_call x3, Pallas kernels, exchange_all(): pl.pallas_call(exchange_body, name='exchange_all', out_shape=jax.ShapeDty...  58.4 us
    unnamed x311, local copies, waits for them, and re-layouts  55.3 us
    pallas_call x1, Pallas kernels, pair_swap(): pl.pallas_call(pair_body, name='pair_swap', out_shape=jax.ShapeDtypeStruc...  54.6 us
    dot_general x18, matrix products, dot_float(): return jnp.dot(left, right, preferred_element_type=jnp.float32)  42.1 us
    dot_general x16, matrix products, dot_t(): lax.dot_general(left, right, (((1,), (1,)), ((), ())), preferred_element_...  34 us
    pallas_call x1, Pallas kernels, swap_both(): pl.pallas_call(swap_both_body, name='swap_both', out_shape=(jax.ShapeDtyp...  33.8 us
  transfers between devices with their start and end apart: 11, of which 1 were waited for; matrix products, arithmetic and copies ran while one was open for 24% of the time, Pallas kernels for 57%

profile of v2, /device:TPU:0, one launch (start us, length us, event | category | flops | bytes accessed | tf_op | source)
XLA Modules:
  0.0 738.2 jit_solution(4150218073730533092)
XLA Ops:
  12.1 3.1 collective-permute-start.2
  18.8 22.6 %swap_dp.1 = bf16[16,24,912]{2,1,0:T(8,128)(2,1)} custom-call(bf16[16,24,912]{2,1,0:T(8,128)(2,1)} %pad_maximum_fusion.4.x_ref), custom_call_target="tpu_custom_call" | custom-call | tf_op jit(solution)/shard_map/swap_dp/pallas_call | solution.py:271
  51.1 28.8 %all-gather.6.cloned.1.call-done = bf16[4,768,768]{2,1,0:T(8,128)(2,1)} async-done(((bf16[4,48,768]{2,1,0:T(8,128)(2,1)}), bf16[4,768,768]{2,1,0:T(8,128)(2,1)}) %all-gather.6.cloned.1.call-update) | async-done | bytes 4718608 | tf_op jit(solution)/shard_map/all_gather | solution.py:1329
  79.9 3.2 convolution_convert_fusion.17
  83.1 4.4 collective-permute-start
  93.6 32.2 %exchange_all.3 = f32[32,24,98]{2,1,0:T(8,128)} custom-call(f32[32,24,98]{2,1,0:T(8,128)} %copy_bitcast_fusion.4.x_ref), custom_call_target="tpu_custom_call" | custom-call | tf_op jit(solution)/shard_map/exchange_all/pallas_call | solution.py:398
  128.2 50.1 %gather_all.2 = bf16[3,32,8,3200]{3,2,1,0:T(8,128)(2,1)} custom-call(bf16[3,8,3200]{2,1,0:T(8,128)(2,1)} %copy-done.12), custom_call_target="tpu_custom_call" | custom-call | tf_op jit(solution)/shard_map/gather_all/pallas_call | solution.py:160
  178.3 4.4 stem_conv.2
  184.7 68.9 %gather_all.3 = bf16[3,32,8,3200]{3,2,1,0:T(8,128)(2,1)} custom-call(bf16[3,8,3200]{2,1,0:T(8,128)(2,1)} %copy-done.13), custom_call_target="tpu_custom_call" | custom-call | tf_op jit(solution)/shard_map/gather_all/pallas_call | solution.py:160
  253.6 5.3 stem_conv.3
  260.9 14.0 %exchange_all.4 = bf16[32,24,196]{2,1,0:T(8,128)(2,1)} custom-call(bf16[32,24,196]{2,1,0:T(8,128)(2,1)} %bitcast.481), custom_call_target="tpu_custom_call" | custom-call | tf_op jit(solution)/shard_map/exchange_all/pallas_call | solution.py:398
  282.9 13.1 %self_attend.1 = (bf16[512,768]{1,0:T(8,128)(2,1)S(1)}, f32[6,8,512]{2,1,0:T(8,128)S(1)}) custom-call(s32[2]{0:T(128)S(1)} %pad_add_fusion.info_ref, f32[8,128]{1,0:T(8,128)S(1)} %broadcast_in_dim.22.ok_ref, bf16[512,768]{1,0:T(8,128)(2,1)S(1)} %fusion.89.q_ref, bf16[1024,768]{1,0:T(8,128)(2,1)S(1)} %pad_maximum_fusion.k_ref, ...), custom_call_target="tpu_custom_call" | custom-call | flops 1610612736 | bytes 4718592 | tf_op jit(solution)/shard_map/self_attend/pallas_call | solution.py:1208
  307.9 6.6 cross_attend.1
  328.1 3.7 convolution_convert_fusion
  348.8 8.5 %copy.301 = bf16[96,8,8,768]{3,1,2,0:T(8,128)(2,1)} copy(bf16[96,8,8,768]{3,1,0,2:T(8,128)(2,1)} %bitcast.373) | data formatting | bytes 18874368
  368.5 3.1 multiply_reduce_fusion
  375.7 7.8 %cross_attend_back.1 = (bf16[512,768]{1,0:T(8,128)(2,1)S(1)}, f32[256,768]{1,0:T(8,128)S(1)}, f32[256,768]{1,0:T(8,128)S(1)}) custom-call(s32[2]{0:T(128)S(1)} %pad_add_fusion.info_ref, f32[256,128]{1,0:T(8,128)S(1)} %copy-done.15, bf16[512,768]{1,0:T(8,128)(2,1)S(1)} %copy-done.30, bf16[256,768]{1,0:T(8,128)(2,1)S(1)} %copy-done.26, ...), custom_call_target="tpu_custom_call" | custom-call | flops 1006632960 | bytes 4718592 | tf_op jit(solution)/shard_map/cross_attend_back/pallas_call | solution.py:1234
  383.6 3.2 multiply_reduce_fusion.1
  390.6 22.7 %self_attend_back.1 = (bf16[512,768]{1,0:T(8,128)(2,1)S(1)}, f32[1024,768]{1,0:T(8,128)}, f32[1024,768]{1,0:T(8,128)}) custom-call(s32[2]{0:T(128)S(1)} %pad_add_fusion.info_ref, f32[8,128]{1,0:T(8,128)S(1)} %broadcast_in_dim.22.ok_ref, bf16[512,768]{1,0:T(8,128)(2,1)S(1)} %copy-done.34, bf16[1024,768]{1,0:T(8,128)(2,1)S(1)} %pad_maximum_fusion.k_ref, ...), custom_call_target="tpu_custom_call" | custom-call | flops 4026531840 | bytes 11796480 | tf_op jit(solution)/shard_map/self_attend_back/pallas_call | solution.py:1234
  423.4 54.6 %pair_swap.1 = bf16[114,1536]{1,0:T(8,128)(2,1)} custom-call(bf16[114,1536]{1,0:T(8,128)(2,1)} %pad_maximum_fusion.11.x_ref), custom_call_target="tpu_custom_call" | custom-call | tf_op jit(solution)/shard_map/pair_swap/pallas_call | solution.py:429
  492.3 3.4 fusion.81
  495.7 3.3 fusion.83
  499.0 8.6 %copy.303 = bf16[96,8,8,768]{3,1,2,0:T(8,128)(2,1)} copy(bf16[96,8,8,768]{3,1,0,2:T(8,128)(2,1)} %bitcast.371) | data formatting | bytes 18874368
  508.1 7.6 %reshape.440.p_ref = bf16[3136,768]{1,0:T(8,128)(2,1)} reshape(bf16[32,98,768]{2,1,0:T(8,128)(2,1)} %all-gather.12.cloned.1.call-done) | data formatting | bytes 9633792
  521.2 12.2 %exchange_all.5 = bf16[32,24,98]{2,1,0:T(8,128)(2,1)} custom-call(bf16[32,24,98]{2,1,0:T(8,128)(2,1)} %copy_bitcast_fusion.5.x_ref), custom_call_target="tpu_custom_call" | custom-call | tf_op jit(solution)/shard_map/exchange_all/pallas_call | solution.py:398
  534.7 7.9 %stem_conv_back.2 = (bf16[768,3200]{1,0:T(8,128)(2,1)}, bf16[216,768]{1,0:T(8,128)(2,1)S(1)}, f32[24,128]{1,0:T(8,128)S(1)}) custom-call(f32[24,3200]{1,0:T(8,128)S(1)} %pad_convert_fusion.dy_ref, f32[24,3200]{1,0:T(8,128)S(1)} %copy-done.11, f32[24,128]{1,0:T(8,128)S(1)} %copy-done.19, f32[24,128]{1,0:T(8,128)S(1)} %pad.26.gb_ref, ...), custom_call_target="tpu_custom_call" | custom-call | tf_op jit(solution)/shard_map/stem_conv_back/pallas_call | solution.py:613
  545.1 45.7 %reduce_all.2 = f32[3,8,3200]{2,1,0:T(8,128)S(1)} custom-call(bf16[3,32,8,3200]{3,2,1,0:T(8,128)(2,1)S(1)} %bitcast.436), custom_call_target="tpu_custom_call" | custom-call | tf_op jit(solution)/shard_map/reduce_all/pallas_call | solution.py:228
  590.9 7.8 %stem_conv_back.3 = (bf16[768,3200]{1,0:T(8,128)(2,1)}, bf16[216,768]{1,0:T(8,128)(2,1)S(1)}, f32[24,128]{1,0:T(8,128)S(1)}) custom-call(f32[24,3200]{1,0:T(8,128)S(1)} %bitcast_add_fusion.1.dy_ref, f32[24,3200]{1,0:T(8,128)S(1)} %copy-done.9, f32[24,128]{1,0:T(8,128)S(1)} %copy-done.17, f32[24,128]{1,0:T(8,128)S(1)} %pad.26.gb_ref, ...), custom_call_target="tpu_custom_call" | custom-call | tf_op jit(solution)/shard_map/stem_conv_back/pallas_call | solution.py:613
  604.0 43.9 %reduce_all.3 = f32[3,8,3200]{2,1,0:T(8,128)S(1)} custom-call(bf16[3,32,8,3200]{3,2,1,0:T(8,128)(2,1)S(1)} %bitcast.435), custom_call_target="tpu_custom_call" | custom-call | tf_op jit(solution)/shard_map/reduce_all/pallas_call | solution.py:228
  662.8 3.2 fusion.88
  674.5 2.9 fusion.116
  680.4 33.8 %swap_both.1 = (bf16[2,16,24,966]{3,2,1,0:T(8,128)(2,1)}, bf16[2,16,24,768]{3,2,1,0:T(8,128)(2,1)}) custom-call(bf16[16,24,966]{2,1,0:T(8,128)(2,1)} %concatenate.67.x_ref, bf16[16,24,768]{2,1,0:T(8,128)(2,1)} %pad_maximum_fusion.5.half_ref), custom_call_target="tpu_custom_call" | custom-call | tf_op jit(solution)/shard_map/swap_both/pallas_call | solution.py:350
  (544 shorter events, 178.8 us)
Async XLA Ops:
  7.2 72.7 %all-gather.6.cloned.1.call-start = ((), (), s32[]{:S(2)}) async-start(), calls=%async_computation.2 | async-start | bytes 5013504 | tf_op jit(solution)/shard_map/all_gather | solution.py:1329
  10.2 265.9 %all-gather.10.cloned.1.call-start = ((), (), s32[]{:S(2)}) async-start(), calls=%async_computation.4 | async-start | bytes 5013504 | tf_op jit(solution)/shard_map/all_gather | solution.py:1339
  10.9 286.9 %all-gather.8.cloned.1.call-start = ((), (), s32[]{:S(2)}) async-start(), calls=%async_computation.3 | async-start | bytes 11280384 | tf_op jit(solution)/shard_map/all_gather | solution.py:1333
  12.0 496.0 %all-gather.12.cloned.1.call-start = ((), (), s32[]{:S(2)}) async-start(), calls=%async_computation.5 | async-start | bytes 5271552 | tf_op jit(solution)/shard_map/all_gather | solution.py:1354
  12.1 38.6 %collective-permute-start.2 = (bf16[16,768]{1,0:T(8,128)(2,1)S(1)}, bf16[16,768]{1,0:T(8,128)(2,1)S(1)}, u32[]{:S(2)}, u32[]{:S(2)}) collective-permute-start(bf16[16,768]{1,0:T(8,128)(2,1)S(1)} %bitcast.529), channel_id=1, source_target_pairs={{0,1},{1,0},{2,3},{3,2},{4,5},{5,4},{6,7},{7,6},{8,9},{9,8},{10,11... | collective-permute-start | bytes 73736 | tf_op jit(solution)/shard_map/ppermute | solution.py:1378
  18.8 25.4 %copy-start.42 = (bf16[1,512,768]{2,1,0:T(8,128)(2,1)S(1)}, bf16[1,512,768]{2,1,0:T(8,128)(2,1)}, u32[]{:S(2)}) copy-start(bf16[1,512,768]{2,1,0:T(8,128)(2,1)} %param.17) | copy-start | bytes 2359300
  44.4 232.9 %copy-start.96 = (f32[512]{0:T(512)}, f32[512]{0:T(512)S(1)}, u32[]{:S(2)}) copy-start(f32[512]{0:T(512)S(1)} %broadcast_multiply_fusion.2) | copy-start | bytes 6148
  44.8 232.5 %copy-start.111 = (f32[512]{0:T(512)}, f32[512]{0:T(512)S(1)}, u32[]{:S(2)}) copy-start(f32[512]{0:T(512)S(1)} %fusion.132) | copy-start | bytes 6148
  45.5 231.8 %copy-start.123 = (f32[768]{0:T(1024)}, f32[768]{0:T(1024)S(1)}, u32[]{:S(2)}) copy-start(f32[768]{0:T(1024)S(1)} %add.291) | copy-start | bytes 9220
  45.6 231.8 %copy-start.90 = (f32[768]{0:T(1024)}, f32[768]{0:T(1024)S(1)}, u32[]{:S(2)}) copy-start(f32[768]{0:T(1024)S(1)} %mul.412) | copy-start | bytes 9220
  83.1 8.9 %copy-start.85 = (bf16[1,98,768]{2,1,0:T(8,128)(2,1)S(1)}, bf16[1,98,768]{2,1,0:T(8,128)(2,1)}, u32[]{:S(2)}) copy-start(bf16[1,98,768]{2,1,0:T(8,128)(2,1)} %param.18) | copy-start | bytes 451588
  83.1 196.5 %collective-permute-start = (bf16[512,768]{1,0:T(8,128)(2,1)}, bf16[512,768]{1,0:T(8,128)(2,1)}, u32[]{:S(2)}, u32[]{:S(2)}) collective-permute-start(bf16[512,768]{1,0:T(8,128)(2,1)} %convolution_convert_fusion.17), channel_id=1, source_target_pairs={{0,1},{2,3},{4,5},{6,7},{8,9},{10,11},{12,13},{14,15},{16,17},{18,... | collective-permute-start | bytes 2359304 | tf_op jit(solution)/shard_map/ppermute | solution.py:659
  89.3 192.0 %collective-permute-start.1 = (bf16[512,768]{1,0:T(8,128)(2,1)}, bf16[512,768]{1,0:T(8,128)(2,1)}, u32[]{:S(2)}, u32[]{:S(2)}) collective-permute-start(bf16[512,768]{1,0:T(8,128)(2,1)} %convolution_convert_fusion.16), channel_id=1, source_target_pairs={{0,1},{2,3},{4,5},{6,7},{8,9},{10,11},{12,13},{14,15},{16,17},{18,... | collective-permute-start | bytes 2359304 | tf_op jit(solution)/shard_map/ppermute | solution.py:659
  93.6 33.5 %copy-start.1 = (f32[16,3200]{1,0:T(8,128)S(1)}, f32[16,3200]{1,0:T(8,128)}, u32[]{:S(2)}) copy-start(f32[16,3200]{1,0:T(8,128)} %constant.129.clone.m_ref) | copy-start | bytes 614404
  128.2 50.1 %copy-start.20 = (f32[24,128]{1,0:T(8,128)}, f32[24,128]{1,0:T(8,128)S(1)}, u32[]{:S(2)}) copy-start(f32[24,128]{1,0:T(8,128)S(1)} %get-tuple-element.69.rstd_ref) | copy-start | bytes 36868
  259.5 16.5 %copy-start.10 = (f32[24,3200]{1,0:T(8,128)}, f32[24,3200]{1,0:T(8,128)S(1)}, u32[]{:S(2)}) copy-start(f32[24,3200]{1,0:T(8,128)S(1)} %get-tuple-element.60.n_ref) | copy-start | bytes 921604
  276.1 401.2 %reduce-scatter.7.cloned.1.call-start = ((), (), s32[]{:S(2)}) async-start(), calls=%async_computation.6 | async-start | bytes 9732096
  300.2 14.3 %copy-start.47 = (f32[512,768]{1,0:T(8,128)}, f32[512,768]{1,0:T(8,128)S(1)}, u32[]{:S(2)}) copy-start(f32[512,768]{1,0:T(8,128)S(1)} %get-tuple-element.187) | copy-start | bytes 4718596
  307.7 9.2 %copy-start.29 = (bf16[512,768]{1,0:T(8,128)(2,1)}, bf16[512,768]{1,0:T(8,128)(2,1)S(1)}, u32[]{:S(2)}) copy-start(bf16[512,768]{1,0:T(8,128)(2,1)S(1)} %fusion.90.q_ref) | copy-start | bytes 2359300
  307.9 9.1 %copy-start.14 = (f32[256,128]{1,0:T(8,128)}, f32[256,128]{1,0:T(8,128)S(1)}, u32[]{:S(2)}) copy-start(f32[256,128]{1,0:T(8,128)S(1)} %broadcast_in_dim.24.ok_ref) | copy-start | bytes 393220
  357.4 321.1 %reduce-scatter.9.cloned.1.call-start = ((), (), s32[]{:S(2)}) async-start(), calls=%async_computation.7 | async-start | bytes 9732096
  375.6 7.9 %copy-start.48 = (f32[512,768]{1,0:T(8,128)S(1)}, f32[512,768]{1,0:T(8,128)}, u32[]{:S(2)}) copy-start(f32[512,768]{1,0:T(8,128)} %copy-done.47) | copy-start | bytes 4718596
  416.0 79.7 %collective-permute-start.4 = (bf16[512,768]{1,0:T(8,128)(2,1)}, bf16[512,768]{1,0:T(8,128)(2,1)}, u32[]{:S(2)}, u32[]{:S(2)}) collective-permute-start(bf16[512,768]{1,0:T(8,128)(2,1)} %slice.555), channel_id=1, source_target_pairs={{1,0},{3,2},{5,4},{7,6},{9,8},{11,10},{13,12},{15,14},{17,16},{19,... | collective-permute-start | bytes 2359304 | tf_op jit(solution)/shard_map/ppermute | solution.py:659
  419.7 72.6 %collective-permute-start.3 = (bf16[512,768]{1,0:T(8,128)(2,1)}, bf16[512,768]{1,0:T(8,128)(2,1)}, u32[]{:S(2)}, u32[]{:S(2)}) collective-permute-start(bf16[512,768]{1,0:T(8,128)(2,1)} %slice.556), channel_id=1, source_target_pairs={{1,0},{3,2},{5,4},{7,6},{9,8},{11,10},{13,12},{15,14},{17,16},{19,... | collective-permute-start | bytes 2359304 | tf_op jit(solution)/shard_map/ppermute | solution.py:659
  422.6 57.5 %copy-start.7 = (bf16[512,768]{1,0:T(8,128)(2,1)S(1)}, bf16[512,768]{1,0:T(8,128)(2,1)}, u32[]{:S(2)}) copy-start(bf16[512,768]{1,0:T(8,128)(2,1)} %copy-done.6) | copy-start | bytes 2359300
  422.6 57.5 %copy-start.74 = (bf16[512,768]{1,0:T(8,128)(2,1)S(1)}, bf16[512,768]{1,0:T(8,128)(2,1)}, u32[]{:S(2)}) copy-start(bf16[512,768]{1,0:T(8,128)(2,1)} %copy-done.73) | copy-start | bytes 2359300
  520.0 14.7 %copy-start.11 = (f32[24,3200]{1,0:T(8,128)S(1)}, f32[24,3200]{1,0:T(8,128)}, u32[]{:S(2)}) copy-start(f32[24,3200]{1,0:T(8,128)} %copy-done.10) | copy-start | bytes 921604
  520.0 14.7 %copy-start.19 = (f32[24,128]{1,0:T(8,128)S(1)}, f32[24,128]{1,0:T(8,128)}, u32[]{:S(2)}) copy-start(f32[24,128]{1,0:T(8,128)} %copy-done.18) | copy-start | bytes 36868
  545.1 45.8 %copy-start.9 = (f32[24,3200]{1,0:T(8,128)S(1)}, f32[24,3200]{1,0:T(8,128)}, u32[]{:S(2)}) copy-start(f32[24,3200]{1,0:T(8,128)} %copy-done.8) | copy-start | bytes 921604
  545.1 45.8 %copy-start.17 = (f32[24,128]{1,0:T(8,128)S(1)}, f32[24,128]{1,0:T(8,128)}, u32[]{:S(2)}) copy-start(f32[24,128]{1,0:T(8,128)} %copy-done.16) | copy-start | bytes 36868
  604.0 44.0 %copy-start.21 = (f32[24,128]{1,0:T(8,128)S(1)}, f32[24,128]{1,0:T(8,128)}, u32[]{:S(2)}) copy-start(f32[24,128]{1,0:T(8,128)} %copy-done.20) | copy-start | bytes 36868
  653.7 12.3 %slice-start.2 = ((s8[4718592]{0:T(1024)(128)(4,1)}), s8[4194304]{0:T(1024)(128)(4,1)S(1)}, s32[]{:S(2)}) async-start(s8[4718592]{0:T(1024)(128)(4,1)} %bitcast.484), calls=%async_computation.10 | async-start | bytes 8388608
  (126 other events, 343.3 us)
Sparse Core Ops, SparseCore 0:
  10.9 68.9 all-gather.5
  82.2 65.1 all-gather.9
  150.2 105.6 all-gather.7
  276.2 67.1 all-gather.11
  357.5 153.0 reduce-scatter.6
  517.3 149.6 reduce-scatter.8
